TPU v7x, 128 devices: a whole 4x4x4 slice. The times are simulated.
128 devices in a mesh: node: 32 (over z, x, core), freq: 4 (over y).
Axes of the slice: x: 4, y: 4, z: 4, core: 2. Of those that a mesh axis runs over, the one named last changes fastest.
Arguments:
- receiver_gathers: float32 [256, 393216], P('node', 'freq'), may hold values from -6 to 6
- fourier_estimate: float32 [256, 2, 256, 384], P(('node', 'freq')), may hold values from -6 to 6
- random_projector: float32 [384, 48], replicated, may hold values from -0.3125 to 0.3125
- release_sample: int32 [384], P('freq'), may hold values from 0 to 393215, as said below
Outputs:
- deblended: float32 [256, 2, 256, 384], P(('node', 'freq'))
- misfit_signal: float32 [256, 393216], P('node', 'freq')
Inputs may be any that keep to these rules, and one draw needn't show every extreme that they name: `release_sample`: shot s fires at a sample of [s * 1024, (s + 1) * 1024).
All inputs are finite; a program needn't handle non-finite values.
Results may differ from a plain program's by a relative error of at most 0.0003.
Values sent between devices are 32-bit elements; how exact they have to be, the bound alone decides.
No kernel may reach another device: no remote copies, remote signals or barrier semaphores. Data moves between devices by JAX's collectives and lax.ppermute only.
A program may use at most 128 MiB of HBM per device.

v0:
```python
import functools
import math

import jax
import jax.numpy as jnp
from jax import lax
from jax.experimental import pallas as pl
from jax.experimental.pallas import tpu as pltpu
from jax.sharding import PartitionSpec as P

SPAN = 4096
FRAME = 1024
RANK = 48
HALO = 4
SHOTS = 96
NODES = 8
EXT = SHOTS + 2 * HALO
FRAMES = SHOTS + HALO
GROUP = 128
RELAX = 0.25
RIDGE = 0.001
highest = lax.Precision.HIGHEST
f32 = jnp.float32
bf16 = jnp.bfloat16


def split(x):
    hi = x.astype(bf16)
    lo = (x - hi.astype(f32)).astype(bf16)
    return hi, lo


def pack_kernel(x_ref, o_ref):
    groups, count = x_ref.shape[0], x_ref.shape[1]
    x = x_ref[...].reshape(groups * count * NODES, 4 * SHOTS)
    lane = lax.broadcasted_iota(jnp.int32, (groups * count * NODES, 128), 1)
    for q in range(4):
        y = pltpu.roll(x, (HALO - SHOTS * q) % (4 * SHOTS), axis=1)[:, :128]
        if q == 0:
            y = jnp.where(lane < HALO, 0.0, y)
        if q == 3:
            y = jnp.where(lane >= HALO + SHOTS, 0.0, y)
        y = y.reshape(groups, count, NODES, 128)
        for g in range(groups):
            o_ref[:, q, g] = y[g]


def pack(x):
    step = 8
    return pl.pallas_call(
        pack_kernel,
        grid=(32 // step,),
        in_specs=[pl.BlockSpec((4, step, NODES, 4 * SHOTS), lambda i: (0, i, 0, 0))],
        out_specs=pl.BlockSpec((step, 4, 4, NODES, 128), lambda i: (i, 0, 0, 0, 0)),
        out_shape=jax.ShapeDtypeStruct((32, 4, 4, NODES, 128), f32),
        name="pack",
    )(x)


def signal_kernel(
    d_ref, last_ref, recv_ref, cos_ref, sin_ref, fh_ref, fl_ref, ah_ref, al_ref, head_ref, gath_ref,
    mis_ref, send_ref,
    c_ref, g_ref, q_ref, dr_ref, lh_ref, ll_ref, mh_ref, ml_ref, sp_ref, in_sem, out_sem,
):
    rows_ext = EXT * NODES
    rows_frames = FRAMES * NODES
    rows_local = SHOTS * NODES

    @pl.loop(0, SHOTS)
    def _(f):
        pltpu.make_async_copy(
            gath_ref.at[:, pl.ds(pl.multiple_of(f * FRAME, FRAME), FRAME)],
            g_ref.at[pl.ds(pl.multiple_of(f * NODES, NODES), NODES), :],
            in_sem,
        ).start()

    for f in range(HALO):
        g_ref[rows_local + f * NODES : rows_local + (f + 1) * NODES, :] = head_ref[
            :, f * FRAME : (f + 1) * FRAME
        ]

    @pl.loop(0, EXT)
    def _(s):
        dr_ref[pl.ds(pl.multiple_of(s * NODES, NODES), NODES), :] = jnp.full((NODES, 128), d_ref[s], jnp.int32)

    @pl.loop(0, NODES)
    def _(n):
        for j in range(2):
            re = recv_ref[pl.ds(2 * j * NODES + n, GROUP, stride=32), :].T[:EXT]
            im = recv_ref[pl.ds((2 * j + 1) * NODES + n, GROUP, stride=32), :].T[:EXT]
            co = cos_ref[:, j * 128 : (j + 1) * 128]
            si = sin_ref[:, j * 128 : (j + 1) * 128]
            c_ref[pl.ds(2 * j * rows_ext + n, EXT, stride=NODES), :] = 2.0 * (re * co + im * si)
            c_ref[pl.ds((2 * j + 1) * rows_ext + n, EXT, stride=NODES), :] = 2.0 * (im * co - re * si)

    step = 80
    parity = 1.0 - 2.0 * (lax.broadcasted_iota(jnp.int32, (step, 128), 1) & 1).astype(f32)

    @pl.loop(0, rows_frames // step)
    def _(i):
        base = pl.multiple_of(i * step, NODES)

        def shot(m, a):
            return c_ref[pl.ds(pl.multiple_of(a * rows_ext + base + (HALO - m) * NODES, NODES), step), :]

        parts = [
            (shot(0, 0) - shot(2, 0)) - parity * (shot(1, 1) - shot(3, 1)),
            (shot(0, 1) - shot(2, 1)) + parity * (shot(1, 0) - shot(3, 0)),
            (shot(0, 2) + shot(2, 2)) - parity * (shot(1, 2) + shot(3, 2)),
            (shot(0, 3) + shot(2, 3)) - parity * (shot(1, 3) + shot(3, 3)),
        ]
        for a in range(4):
            hi, lo = split(parts[a])
            lh_ref[pl.ds(base, step), a * 128 : (a + 1) * 128] = hi
            ll_ref[pl.ds(base, step), a * 128 : (a + 1) * 128] = lo

    @pl.loop(0, rows_ext // 64)
    def _(i):
        base = pl.multiple_of(i * 64, 64)
        target = pl.multiple_of(rows_frames + base, 32)
        for a in range(4):
            hi, lo = split(c_ref[pl.ds(pl.multiple_of(a * rows_ext + base, 64), 64), :])
            lh_ref[pl.ds(target, 64), a * 128 : (a + 1) * 128] = hi
            ll_ref[pl.ds(target, 64), a * 128 : (a + 1) * 128] = lo

    def product(hi, lo, th, tl):
        out = jnp.dot(hi, th, preferred_element_type=f32)
        out += jnp.dot(lo, th, preferred_element_type=f32)
        return out + jnp.dot(hi, tl, preferred_element_type=f32)

    width = 256
    half = rows_ext // 2

    @pl.loop(0, 2 * (FRAME // width))
    def _(i):
        m = i // (FRAME // width)
        c = i % (FRAME // width)
        col = pl.multiple_of(c * width, width)
        row = pl.multiple_of(rows_frames + m * half, 16)
        out = product(
            lh_ref[pl.ds(row, half), :], ll_ref[pl.ds(row, half), :],
            fh_ref[:, pl.ds(col, width)], fl_ref[:, pl.ds(col, width)],
        )
        dest = pl.multiple_of(m * half, 16)
        lane = lax.broadcasted_iota(jnp.int32, (half, 128), 1)
        shift = dr_ref[pl.ds(dest, half), :] - col
        for k in range(width // 128):
            q_ref[pl.ds(dest, half), pl.ds(pl.multiple_of(col + k * 128, 128), 128)] = jnp.where(
                lane + k * 128 < shift, out[:, k * 128 : (k + 1) * 128], 0.0
            )

    pltpu.make_async_copy(g_ref.at[pl.ds(0, rows_local), :], g_ref.at[pl.ds(0, rows_local), :], in_sem).wait()
    half_f = rows_frames // 2

    @pl.loop(0, 2 * (FRAME // width))
    def _(i):
        m = i // (FRAME // width)
        c = i % (FRAME // width)
        col = pl.multiple_of(c * width, width)
        row = pl.multiple_of(m * half_f, 16)
        out = product(
            lh_ref[pl.ds(row, half_f), :], ll_ref[pl.ds(row, half_f), :],
            fh_ref[:, pl.ds(col, width)], fl_ref[:, pl.ds(col, width)],
        )
        cols = pl.ds(col, width)
        lead = pl.multiple_of(row + HALO * NODES, 16)
        g_ref[pl.ds(row, half_f), cols] = (
            g_ref[pl.ds(row, half_f), cols] - out + q_ref[pl.ds(lead, half_f), cols] - q_ref[pl.ds(row, half_f), cols]
        )

    @pl.when(last_ref[0] > 0)
    def _():
        g_ref[rows_local:rows_frames, :] = jnp.zeros((HALO * NODES, FRAME), f32)

    @pl.loop(0, SHOTS)
    def _(f):
        pltpu.make_async_copy(
            g_ref.at[pl.ds(pl.multiple_of(f * NODES, NODES), NODES), :],
            mis_ref.at[:, pl.ds(pl.multiple_of(f * FRAME, FRAME), FRAME)],
            out_sem,
        ).start()

    @pl.loop(0, rows_frames // 32)
    def _(i):
        base = pl.multiple_of(i * 32, 32)
        hi, lo = split(g_ref[pl.ds(base, 32), :])
        mh_ref[pl.ds(base, 32), :] = hi
        ml_ref[pl.ds(base, 32), :] = lo

    @pl.loop(0, rows_local // 32)
    def _(i):
        base = pl.multiple_of(i * 32, 32)
        lead = pl.multiple_of(base + HALO * NODES, 32)
        target = pl.multiple_of(rows_frames + base, 32)
        shift = dr_ref[pl.ds(lead, 32), :]
        lane = lax.broadcasted_iota(jnp.int32, (32, 128), 1)
        for k in range(FRAME // 128):
            cols = slice(k * 128, (k + 1) * 128)
            diff = jnp.where(lane + k * 128 < shift, g_ref[pl.ds(lead, 32), cols] - g_ref[pl.ds(base, 32), cols], 0.0)
            hi, lo = split(diff)
            mh_ref[pl.ds(target, 32), cols] = hi
            ml_ref[pl.ds(target, 32), cols] = lo

    total = rows_frames + rows_local
    quarter = total // 7

    @pl.loop(0, 7 * 2)
    def _(i):
        row = pl.multiple_of((i // 2) * quarter, 32)
        col = pl.multiple_of((i % 2) * 256, 256)
        out = product(
            mh_ref[pl.ds(row, quarter), :], ml_ref[pl.ds(row, quarter), :],
            ah_ref[:, pl.ds(col, 256)], al_ref[:, pl.ds(col, 256)],
        )
        for k in range(2):
            place = pl.multiple_of(((i % 2) * 2 + k) * total + row, 32)
            sp_ref[pl.ds(place, quarter), :] = out[:, k * 128 : (k + 1) * 128]

    sign = 1.0 - 2.0 * (lax.broadcasted_iota(jnp.int32, (SHOTS, 128), 1) & 1).astype(f32)

    @pl.loop(0, NODES)
    def _(n):
        def frame(m, a):
            return sp_ref[pl.ds(a * total + m * NODES + n, SHOTS, stride=NODES), :]

        def edge(a):
            return sp_ref[pl.ds(a * total + rows_frames + n, SHOTS, stride=NODES), :]

        parts = [
            (frame(0, 0) - frame(2, 0)) + sign * (frame(1, 1) - frame(3, 1)) + edge(0),
            (frame(0, 1) - frame(2, 1)) - sign * (frame(1, 0) - frame(3, 0)) + edge(1),
            (frame(0, 2) + frame(2, 2)) - sign * (frame(1, 2) + frame(3, 2)) + edge(2),
            (frame(0, 3) + frame(2, 3)) - sign * (frame(1, 3) + frame(3, 3)) + edge(3),
        ]
        outs = []
        for j in range(2):
            co = RELAX * cos_ref[HALO : HALO + SHOTS, j * 128 : (j + 1) * 128]
            si = RELAX * sin_ref[HALO : HALO + SHOTS, j * 128 : (j + 1) * 128]
            re, im = parts[2 * j], parts[2 * j + 1]
            outs += [re * co - im * si, im * co + re * si]
        for a in range(3):
            block = jnp.concatenate([outs[a], outs[3][32 * a : 32 * a + 32]], 0).T
            send_ref[pl.ds(a * NODES + n, GROUP, stride=24), :] = block

    pltpu.make_async_copy(g_ref.at[pl.ds(0, rows_local), :], g_ref.at[pl.ds(0, rows_local), :], out_sem).wait()


def signal(dither, last, recv, cos_t, sin_t, tables, head, gathers):
    vmem = pl.BlockSpec(memory_space=pltpu.VMEM)
    smem = pl.BlockSpec(memory_space=pltpu.SMEM)
    hbm = pl.BlockSpec(memory_space=pltpu.HBM)
    rows_ext, rows_frames, rows_local = EXT * NODES, FRAMES * NODES, SHOTS * NODES
    return pl.pallas_call(
        signal_kernel,
        in_specs=[smem, smem, vmem, vmem, vmem, vmem, vmem, vmem, vmem, vmem, hbm],
        out_specs=[hbm, vmem],
        out_shape=[
            jax.ShapeDtypeStruct((NODES, SHOTS * FRAME), f32),
            jax.ShapeDtypeStruct((GROUP * 24, 128), f32),
        ],
        scratch_shapes=[
            pltpu.VMEM((4 * rows_ext, 128), f32),
            pltpu.VMEM((rows_frames, FRAME), f32),
            pltpu.VMEM((rows_ext, FRAME), f32),
            pltpu.VMEM((rows_ext, 128), jnp.int32),
            pltpu.VMEM((rows_frames + rows_ext, 512), bf16),
            pltpu.VMEM((rows_frames + rows_ext, 512), bf16),
            pltpu.VMEM((rows_frames + rows_local, FRAME), bf16),
            pltpu.VMEM((rows_frames + rows_local, FRAME), bf16),
            pltpu.VMEM((4 * (rows_frames + rows_local), 128), f32),
            pltpu.SemaphoreType.DMA,
            pltpu.SemaphoreType.DMA,
        ],
        compiler_params=pltpu.CompilerParams(vmem_limit_bytes=56 << 20),
        name="signal",
    )(dither, last, recv, cos_t, sin_t, *tables, head, gathers)


def rank_kernel(recv_ref, est_ref, wr_ref, wi_ref, out_ref, a_ref, y_ref, c_ref, s_ref):
    lane = lax.broadcasted_iota(jnp.int32, (NODES, 128), 1)
    chunk = lane // 32

    @pl.loop(0, 32)
    def _(p):
        rows = pl.ds(pl.multiple_of(p * NODES, NODES), NODES)
        extras = []
        for a in range(3):
            t = []
            for q in range(4):
                tile = recv_ref[pl.ds(pl.multiple_of((p * 4 + q) * 24 + a * NODES, NODES), NODES), :]
                t.append(pltpu.roll(tile, (96 * q) % 128, axis=1) if q else tile)
            v = [
                jnp.where(lane < 96, t[0], t[1]),
                jnp.where(lane < 64, t[1], t[2]),
                jnp.where(lane < 32, t[2], t[3]),
            ]
            for i in range(3):
                cols = slice(i * 128, (i + 1) * 128)
                a_ref[a, rows, cols] = est_ref[a, rows, cols] + v[i]
            e = jnp.where(chunk == 0, t[3], jnp.where(chunk == 1, t[2], jnp.where(chunk == 2, t[1], t[0])))
            extras.append(pltpu.roll(e, 32 * (a + 1), axis=1))
        for i in range(3):
            cols = slice(i * 128, (i + 1) * 128)
            x = extras[(4 * i) % 3]
            for k in range(1, 4):
                x = jnp.where(chunk == k, extras[(4 * i + k) % 3], x)
            a_ref[3, rows, cols] = est_ref[3, rows, cols] + x

    dot = functools.partial(jnp.dot, precision=highest, preferred_element_type=f32)

    def dot_t(x, y):
        return lax.dot_general(x, y, (((0,), (0,)), ((), ())), precision=highest, preferred_element_type=f32)

    def dot_nt(x, y):
        return lax.dot_general(x, y, (((1,), (1,)), ((), ())), precision=highest, preferred_element_type=f32)

    lane_r = lax.broadcasted_iota(jnp.int32, (64, 128), 1)
    row_r = lax.broadcasted_iota(jnp.int32, (64, 128), 0)
    flip = jnp.where(lane_r < 64, 1.0, -1.0).astype(f32)
    diagonal = (lane_r == row_r) & (row_r < RANK)
    systems = []
    for j in range(2):
        re, im = a_ref[2 * j], a_ref[2 * j + 1]
        y = dot(re, wr_ref[...]) + dot(im, wi_ref[...])
        y_ref[j] = y
        ya = y[:, :128]
        g = dot_t(ya, ya)
        g = g[:64] + flip * pltpu.roll(g[64:], 64, axis=1)
        trace = jnp.sum(jnp.where(diagonal, g, 0.0))
        g = jnp.where(diagonal, g + RIDGE * trace / RANK, g)
        eye = jnp.where(diagonal, 1.0, 0.0).astype(f32)
        systems.append([g[: RANK], eye[: RANK]])
        dr = dot_t(ya, re)
        di = dot_t(ya, im)
        c_ref[j, :64] = dr[:64] + di[64:]
        c_ref[j, 64:] = di[:64] - dr[64:]

    neg = jnp.where(lax.broadcasted_iota(jnp.int32, (1, 128), 1) < 64, -1.0, 1.0).astype(f32)
    row_i = lax.broadcasted_iota(jnp.int32, (RANK, 128), 0)
    for k in range(RANK - 1):
        start = ((k + 1) // 8) * 8
        for j in range(2):
            g, w = systems[j]
            gk, wk = g[k : k + 1], w[k : k + 1]
            inv = 1.0 / gk[:, k : k + 1]
            gk, wk = gk * inv, wk * inv
            gs, ws = neg * pltpu.roll(gk, 64, axis=1), neg * pltpu.roll(wk, 64, axis=1)
            below = g[start:]
            live = row_i[start:] > k
            cr = jnp.where(live, below[:, k : k + 1], 0.0)
            ci = jnp.where(live, below[:, 64 + k : 65 + k], 0.0)
            low_g = below - (cr * gk + ci * gs)
            low_w = w[start:] - (cr * wk + ci * ws)
            if start:
                low_g = jnp.concatenate([g[:start], low_g], 0)
                low_w = jnp.concatenate([w[:start], low_w], 0)
            systems[j] = [low_g, low_w]

    for j in range(2):
        g, w = systems[j]
        d = jnp.sum(jnp.where(diagonal[:RANK], g, 0.0), axis=1, keepdims=True)
        w = w * lax.rsqrt(d)
        w = jnp.concatenate([w, jnp.zeros((16, 128), f32)], 0)
        zero = jnp.zeros((64, 128), f32)
        left = jnp.concatenate([flip * w, pltpu.roll(w, 64, axis=1)], 0)
        v = dot(left, c_ref[j])
        big = jnp.concatenate(
            [
                jnp.concatenate([w, zero], 1), jnp.concatenate([zero, w], 1),
                jnp.concatenate([zero, -w], 1), jnp.concatenate([w, zero], 1),
            ], 0,
        )
        z = dot_nt(y_ref[j], big)
        out_ref[2 * j] = dot(z[:, :128], v)
        out_ref[2 * j + 1] = dot(z[:, 128:], v)


def rank_reduce(recv, est, wr, wi):
    vmem = pl.BlockSpec(memory_space=pltpu.VMEM)
    return pl.pallas_call(
        rank_kernel,
        in_specs=[vmem] * 4,
        out_specs=vmem,
        out_shape=jax.ShapeDtypeStruct((4, 256, 384), f32),
        scratch_shapes=[
            pltpu.VMEM((4, 256, 384), f32),
            pltpu.VMEM((2, 256, 256), f32),
            pltpu.VMEM((2, 128, 384), f32),
            pltpu.VMEM((8, 128), f32),
        ],
        compiler_params=pltpu.CompilerParams(vmem_limit_bytes=56 << 20),
        name="rank",
    )(recv, est, wr, wi)


def table(rows_first):
    shape = (512, FRAME) if rows_first else (FRAME, 512)
    row = lax.broadcasted_iota(jnp.int32, shape, 0 if rows_first else 1)
    time = lax.broadcasted_iota(jnp.int32, shape, 1 if rows_first else 0)
    block = row // 128
    k = 2 * (row % 128) + block // 2 + 1
    phase = (k * time + (block % 2) * (SPAN // 4)) % SPAN
    value = jnp.cos(2.0 * math.pi / SPAN * phase.astype(f32)) / math.sqrt(SPAN)
    hi = lax.reduce_precision(value, 8, 7)
    return hi.astype(bf16), (value - hi).astype(bf16)


def shards(receiver_gathers, fourier_estimate, random_projector, release_sample):
    q = lax.axis_index("freq")
    est = fourier_estimate.reshape(4, 32, NODES, 4 * SHOTS)
    send = pack(est).reshape(GROUP, 32, 128)
    recv = lax.all_to_all(send, ("node", "freq"), split_axis=0, concat_axis=0, tiled=True)

    up = [(0, 1), (1, 2), (2, 3)]
    down = [(1, 0), (2, 1), (3, 2)]
    head = lax.ppermute(receiver_gathers[:, : HALO * FRAME], "freq", down)
    release_before = lax.ppermute(release_sample[SHOTS - HALO :], "freq", up)
    release_after = lax.ppermute(release_sample[:HALO], "freq", down)
    dither = jnp.concatenate([release_before, release_sample, release_after]) % FRAME
    src = lax.iota(jnp.int32, 256)
    k = 2 * (src % 128) + src // 128 + 1
    angle = 2.0 * math.pi / SPAN * (k[None, :] * dither[:, None] % SPAN).astype(f32)
    cos_t, sin_t = jnp.cos(angle), jnp.sin(angle)
    tables = table(True) + table(False)
    last = (q == 3).astype(jnp.int32).reshape(1)
    misfit, back = signal(dither, last, recv.reshape(GROUP * 32, 128), cos_t, sin_t, tables, head, receiver_gathers)

    arrived = lax.all_to_all(
        back.reshape(GROUP, 24, 128), ("node", "freq"), split_axis=0, concat_axis=0, tiled=True
    )
    omega = jnp.pad(random_projector, ((0, 0), (0, 16)))
    zero = jnp.zeros_like(omega)
    wr = jnp.concatenate([omega, zero, zero, omega], 1)
    wi = jnp.concatenate([zero, omega, -omega, zero], 1)
    low = rank_reduce(arrived.reshape(GROUP * 24, 128), fourier_estimate.reshape(4, 256, 384), wr, wi)
    return low.reshape(2, 2, 256, 384), misfit


def solution(mesh):
    return jax.shard_map(
        shards,
        mesh=mesh,
        in_specs=(P("node", "freq"), P(("node", "freq"), None, None, None), P(), P("freq")),
        out_specs=(P(("node", "freq"), None, None, None), P("node", "freq")),
        check_vma=False,
    )
```

profile of v0, /device:TPU:1, one launch (start us, length us, event | category | flops | bytes accessed | tf_op | source)
XLA Modules:
  0.0 138.4 jit_solution(14636745567050732592)
XLA Ops:
  0.6 0.8 fusion.47
  1.4 4.0 %collective-permute-start = (s32[4]{0:T(128)S(1)}, s32[4]{0:T(128)S(1)}, u32[]{:S(2)}, u32[]{:S(2)}) collective-permute-start(s32[4]{0:T(128)S(1)} %get-tuple-element.16), channel_id=1, source_target_pairs={{0,1},{1,2},{2,3},{4,5},{5,6},{6,7},{8,9},{9,10},{10,11},{12,13},{... | collective-permute-start | bytes 56 | tf_op jit(solution)/shard_map/ppermute | solution.py:417
  5.4 1.3 collective-permute-start.1
  6.7 4.3 %pack.1 = f32[32,4,4,8,128]{4,3,2,1,0:T(8,128)} custom-call(f32[4,32,8,384]{3,2,1,0:T(8,128)} %bitcast.10), custom_call_target="tpu_custom_call" | custom-call | tf_op jit(solution)/shard_map/pack/pallas_call | solution.py:50
  11.0 12.0 %all-to-all-start = ((f32[128,32,128]{2,1,0:T(8,128)}), f32[128,32,128]{2,1,0:T(8,128)S(1)}, u32[]{:S(2)}, u32[]{:S(2)}) async-start(f32[128,32,128]{2,1,0:T(8,128)} %bitcast.9), calls=%async_computation | async-start | bytes 4194304 | tf_op jit(solution)/shard_map/all_to_all | solution.py:412
  23.1 0.9 slice.11
  24.0 1.3 collective-permute-start.2
  25.3 0.0 copy-start.5
  25.4 9.1 %fusion.1 = (bf16[1024,512]{1,0:T(8,128)(2,1)}, bf16[1024,512]{1,0:T(8,128)(2,1)}) fusion(s32[512]{0:T(512)S(1)} %get-tuple-element.18, s32[512]{0:T(512)S(1)} %get-tuple-element.21, pred[512]{0:T(512)(128)(4,1)S(1)} %get-tuple-element.22, s32[512]{0:T(512)S(1)} %get-tuple-element.19, s32[512]{0:T(512)S(1)} %get-tuple-element.20, ...), kind=kLoop, calls=%fused_computation.27 | loop fusion | flops 23592960 | bytes 2106368 | tf_op jit(solution)/shard_map/convert_element_type | solution.py:405
  34.5 10.1 %fusion = (bf16[512,1024]{1,0:T(8,128)(2,1)}, bf16[512,1024]{1,0:T(8,128)(2,1)}) fusion(s32[512]{0:T(512)S(1)} %get-tuple-element.18, s32[512]{0:T(512)S(1)} %get-tuple-element.21, pred[512]{0:T(512)(128)(4,1)S(1)} %get-tuple-element.22, s32[512]{0:T(512)S(1)} %get-tuple-element.19, s32[512]{0:T(512)S(1)} %get-tuple-element.20, ...), kind=kLoop, calls=%fused_computation.26 | loop fusion | flops 23592960 | bytes 2106368 | tf_op jit(solution)/shard_map/convert_element_type | solution.py:405
  44.6 0.0 collective-permute-done
  44.6 0.0 collective-permute-done.1
  44.6 0.0 copy-done.5
  44.6 0.1 and_select_fusion.2.d_ref
  44.7 0.0 copy-start.4
  44.7 1.2 fusion.33
  45.9 3.8 %collective-permute-done.2.head_ref = f32[8,4096]{1,0:T(8,128)S(1)} collective-permute-done((f32[8,4096]{1,0:T(8,128)S(1)}, f32[8,4096]{1,0:T(8,128)S(1)}, u32[]{:S(2)}, u32[]{:S(2)}) %collective-permute-start.2) | collective-permute-done | bytes 131104 | tf_op jit(solution)/shard_map/ppermute | solution.py:416
  49.7 0.0 copy-start.2
  49.7 3.9 %all-to-all-done = f32[128,32,128]{2,1,0:T(8,128)S(1)} async-done(((f32[128,32,128]{2,1,0:T(8,128)}), f32[128,32,128]{2,1,0:T(8,128)S(1)}, u32[]{:S(2)}, u32[]{:S(2)}) %all-to-all-start) | async-done | bytes 2097184 | tf_op jit(solution)/shard_map/all_to_all | solution.py:412
  53.6 0.0 copy-start
  53.6 0.0 copy-done.4
  53.6 0.0 copy-done.2
  53.6 1.3 copy-done
  54.9 28.9 %signal.1 = (f32[8,98304]{1,0:T(8,128)}, f32[3072,128]{1,0:T(8,128)}) custom-call(s32[104]{0:T(128)} %copy-done.4, s32[1]{0:T(128)} %bitcast.last_ref, f32[4096,128]{1,0:T(8,128)} %bitcast.8, f32[104,256]{1,0:T(8,128)} %get-tuple-element.15.cos_ref, f32[104,256]{1,0:T(8,128)} %get-tuple-element.14.sin_ref, bf16[512,1024]{1,0:T(8,128)(2,1)} %get-tuple-element.13.fh_ref, ...), custom_call_target="tpu_custom_call" | custom-call | tf_op jit(solution)/shard_map/signal/pallas_call | solution.py:253
  83.9 0.0 copy-start.3
  83.9 6.1 %all-to-all-start.1 = ((f32[128,24,128]{2,1,0:T(8,128)}), f32[128,24,128]{2,1,0:T(8,128)S(1)}, u32[]{:S(2)}, u32[]{:S(2)}) async-start(f32[128,24,128]{2,1,0:T(8,128)} %bitcast.13), calls=%async_computation.1 | async-start | bytes 3145728 | tf_op jit(solution)/shard_map/all_to_all | solution.py:428
  89.9 0.0 copy-done.3
  90.0 0.1 copy.6
  90.1 0.1 pad.10.clone
  90.2 1.2 pad_maximum_fusion.1
  91.4 23.4 %all-to-all-done.1 = f32[128,24,128]{2,1,0:T(8,128)S(1)} async-done(((f32[128,24,128]{2,1,0:T(8,128)}), f32[128,24,128]{2,1,0:T(8,128)S(1)}, u32[]{:S(2)}, u32[]{:S(2)}) %all-to-all-start.1) | async-done | bytes 1572896 | tf_op jit(solution)/shard_map/all_to_all | solution.py:428
  114.8 0.0 copy-start.1
  114.8 1.2 copy-done.1
  115.9 22.5 %rank.1 = f32[4,256,384]{2,1,0:T(8,128)} custom-call(f32[3072,128]{1,0:T(8,128)} %bitcast.12, f32[4,256,384]{2,1,0:T(8,128)} %bitcast.11, f32[384,256]{1,0:T(8,128)} %get-tuple-element.7.wr_ref, f32[384,256]{1,0:T(8,128)} %get-tuple-element.6.wi_ref), custom_call_target="tpu_custom_call" | custom-call | tf_op jit(solution)/shard_map/rank/pallas_call | solution.py:380
  (7 shorter events, 0.1 us)
Async XLA Ops:
  1.4 43.2 %collective-permute-start = (s32[4]{0:T(128)S(1)}, s32[4]{0:T(128)S(1)}, u32[]{:S(2)}, u32[]{:S(2)}) collective-permute-start(s32[4]{0:T(128)S(1)} %get-tuple-element.16), channel_id=1, source_target_pairs={{0,1},{1,2},{2,3},{4,5},{5,6},{6,7},{8,9},{9,10},{10,11},{12,13},{... | collective-permute-start | bytes 56 | tf_op jit(solution)/shard_map/ppermute | solution.py:417
  5.4 39.2 %collective-permute-start.1 = (s32[4]{0:T(128)S(1)}, s32[4]{0:T(128)S(1)}, u32[]{:S(2)}, u32[]{:S(2)}) collective-permute-start(s32[4]{0:T(128)S(1)} %get-tuple-element.17), channel_id=1, source_target_pairs={{1,0},{2,1},{3,2},{5,4},{6,5},{7,6},{9,8},{10,9},{11,10},{13,12},{... | collective-permute-start | bytes 56 | tf_op jit(solution)/shard_map/ppermute | solution.py:418
  11.0 42.6 %all-to-all-start = ((f32[128,32,128]{2,1,0:T(8,128)}), f32[128,32,128]{2,1,0:T(8,128)S(1)}, u32[]{:S(2)}, u32[]{:S(2)}) async-start(f32[128,32,128]{2,1,0:T(8,128)} %bitcast.9), calls=%async_computation | async-start | bytes 4194304 | tf_op jit(solution)/shard_map/all_to_all | solution.py:412
  24.0 25.7 %collective-permute-start.2 = (f32[8,4096]{1,0:T(8,128)S(1)}, f32[8,4096]{1,0:T(8,128)S(1)}, u32[]{:S(2)}, u32[]{:S(2)}) collective-permute-start(f32[8,4096]{1,0:T(8,128)S(1)} %slice.11), channel_id=1, source_target_pairs={{1,0},{2,1},{3,2},{5,4},{6,5},{7,6},{9,8},{10,9},{11,10},{13,12},{... | collective-permute-start | bytes 393224 | tf_op jit(solution)/shard_map/ppermute | solution.py:416
  25.3 19.3 %copy-start.5 = (s32[96]{0:T(128)S(1)}, s32[96]{0:T(128)}, u32[]{:S(2)}) copy-start(s32[96]{0:T(128)} %param.7) | copy-start | bytes 1156
  44.7 8.9 %copy-start.4 = (s32[104]{0:T(128)}, s32[104]{0:T(128)S(1)}, u32[]{:S(2)}) copy-start(s32[104]{0:T(128)S(1)} %and_select_fusion.2.d_ref) | copy-start | bytes 1252
  49.7 3.9 %copy-start.2 = (f32[8,4096]{1,0:T(8,128)}, f32[8,4096]{1,0:T(8,128)S(1)}, u32[]{:S(2)}) copy-start(f32[8,4096]{1,0:T(8,128)S(1)} %collective-permute-done.2.head_ref) | copy-start | bytes 393220
  53.6 1.3 copy-start
  83.9 6.1 %copy-start.3 = (f32[384,48]{0,1:T(8,128)S(1)}, f32[384,48]{0,1:T(8,128)}, u32[]{:S(2)}) copy-start(f32[384,48]{0,1:T(8,128)} %param.6) | copy-start | bytes 221188
  83.9 30.9 %all-to-all-start.1 = ((f32[128,24,128]{2,1,0:T(8,128)}), f32[128,24,128]{2,1,0:T(8,128)S(1)}, u32[]{:S(2)}, u32[]{:S(2)}) async-start(f32[128,24,128]{2,1,0:T(8,128)} %bitcast.13), calls=%async_computation.1 | async-start | bytes 3145728 | tf_op jit(solution)/shard_map/all_to_all | solution.py:428
  114.8 1.2 copy-start.1
where the time goes:
time: 139 us; the launch traced here: 138 us
  Pallas kernels  55.7 us (40%)
  waiting for transfers between devices  31.1 us (22%)
  starting transfers between devices  24.7 us (18%)
  other arithmetic  21.7 us (16%)
  local copies, waits for them, and re-layouts  4.44 us (3%)
    pallas_call x1, Pallas kernels, signal(): pl.pallas_call(signal_kernel, in_specs=[smem, smem, vmem, vmem, vmem, vme...  28.9 us
    all_to_all x1, waiting for transfers between devices, shards(): lax.all_to_all(back.reshape(GROUP, 24, 128), ('node', 'freq'), split_axis...  23.4 us
    pallas_call x1, Pallas kernels, rank_reduce(): pl.pallas_call(rank_kernel, in_specs=[vmem] * 4, out_specs=vmem, out_shap...  22.5 us
    convert_element_type x2, other arithmetic, table(): return (hi.astype(bf16), (value - hi).astype(bf16))  19.2 us
    all_to_all x1, starting transfers between devices, shards(): lax.all_to_all(send, ('node', 'freq'), split_axis=0, concat_axis=0, tiled...  12 us
    all_to_all x1, starting transfers between devices, shards(): lax.all_to_all(back.reshape(GROUP, 24, 128), ('node', 'freq'), split_axis...  6.06 us
    pallas_call x1, Pallas kernels, pack(): pl.pallas_call(pack_kernel, grid=(32 // step,), in_specs=[pl.BlockSpec((4...  4.29 us
    ppermute x1, starting transfers between devices, shards(): release_before = lax.ppermute(release_sample[SHOTS - HALO:], 'freq', up)  4.01 us
  transfers between devices with their start and end apart: 5, of which 3 were waited for; matrix products, arithmetic and copies ran while one was open for 17% of the time, Pallas kernels for 3%

commit v1 on v0

v1 whole, which is shorter than its diff:
```python
import functools
import math

import jax
import jax.numpy as jnp
from jax import lax
from jax.experimental import pallas as pl
from jax.experimental.pallas import tpu as pltpu
from jax.sharding import PartitionSpec as P


SPAN = 4096
FRAME = 1024
RANK = 48
HALO = 4
SHOTS = 96
NODES = 8
EXT = SHOTS + 2 * HALO
FRAMES = SHOTS + HALO
GROUP = 128
ROWS = 26
ORDER = (0, 2, 1, 3)
RELAX = 0.25
RIDGE = 0.001
highest = lax.Precision.HIGHEST
f32 = jnp.float32
bf16 = jnp.bfloat16


def split(x):
    hi = x.astype(bf16)
    lo = (x - hi.astype(f32)).astype(bf16)
    return hi, lo


def pack_kernel(x_ref, o_ref):
    count = x_ref.shape[1]
    lane = lax.broadcasted_iota(jnp.int32, (NODES, 128), 1)
    node = lax.broadcasted_iota(jnp.int32, (NODES, 128), 0)
    slot = lane // 32
    own = slot == node % 4

    def turn(v, by):
        return pltpu.roll(v, by % 128, axis=1) if by % 128 else v

    @pl.loop(0, count)
    def _(p):
        x = [[x_ref[a, p, :, i * 128 : (i + 1) * 128] for i in range(3)] for a in range(4)]
        edges = jnp.zeros((NODES, 128), f32)
        for k in range(3):
            for a in range(4):
                moved = turn(x[a][k], 32 * k + 8 * a - (92 - 32 * k))
                edges = jnp.where((slot == k) & ((lane // 8) % 4 == a), moved, edges)
        turned = [turn(edges, 32 * r) for r in range(4)]

        def spread(k):
            v = turned[(0 - k) % 4]
            for m in range(1, 4):
                v = jnp.where(slot == m, turned[(m - k) % 4], v)
            return jnp.where(own, v, 0.0)

        spreads = [spread(k) for k in range(3)]
        zero = jnp.zeros((NODES, 128), f32)
        for q in range(4):
            base = (p * 4 + q) * ROWS
            for a in range(3):
                if q == 0:
                    main = x[a][0]
                elif q == 3:
                    main = turn(x[a][2], 96)
                else:
                    main = jnp.where(lane < 32 * q, turn(x[a][q - 1], 32 * q), turn(x[a][q], 32 * q))
                m = 3 * q + a
                rest = turn(x[3][m // 4], 32 * (3 - m % 4))
                o_ref[pl.ds(base + NODES * a, NODES), :] = jnp.where(lane < SHOTS, main, rest)
            before = spreads[q - 1] if q > 0 else zero
            after = spreads[q] if q < 3 else zero
            halo = jnp.where(lane % 8 < 4, before, after)
            halo = halo + pltpu.roll(halo, 1, axis=0)
            halo = halo + pltpu.roll(halo, 2, axis=0)
            o_ref[pl.ds(base + 24, 1), :] = halo[3:4]
            o_ref[pl.ds(base + 25, 1), :] = halo[7:8]


def pack(x):
    step = 8
    return pl.pallas_call(
        pack_kernel,
        grid=(32 // step,),
        in_specs=[pl.BlockSpec((4, step, NODES, 4 * SHOTS), lambda i: (0, i, 0, 0))],
        out_specs=pl.BlockSpec((step * 4 * ROWS, 128), lambda i: (i, 0)),
        out_shape=jax.ShapeDtypeStruct((GROUP * ROWS, 128), f32),
        compiler_params=pltpu.CompilerParams(vmem_limit_bytes=56 << 20),
        name="pack",
    )(x)


def product(hi, lo, th, tl):
    return jnp.dot(
        jnp.concatenate([hi, lo, hi], 1), jnp.concatenate([th, th, tl], 0), preferred_element_type=f32
    )


def signal_kernel(
    d_ref, last_ref, recv_ref, cos_ref, sin_ref, fh_hbm, fl_hbm, ah_hbm, al_hbm, head_ref, gath_ref,
    mis_ref, send_hbm,
    c_ref, g_ref, q_ref, h_ref, lh_ref, ll_ref, mh_ref, ml_ref, sp_ref, w_ref, send_ref,
    fh_ref, fl_ref, ah_ref, al_ref, in_sem, head_sem, out_sem, send_sem, table_sem,
):
    rows_ext = EXT * NODES
    rows_frames = FRAMES * NODES
    rows_local = SHOTS * NODES
    local = SHOTS * FRAME
    loads = [
        pltpu.make_async_copy(src, dst, table_sem.at[i])
        for i, (src, dst) in enumerate(
            [(fh_hbm, fh_ref), (fl_hbm, fl_ref), (ah_hbm, ah_ref), (al_hbm, al_ref)]
        )
    ]
    loads[0].start()
    loads[1].start()
    fetch = pltpu.make_async_copy(gath_ref, g_ref.at[:, pl.ds(0, local)], in_sem)
    fetch.start()
    fetch_head = pltpu.make_async_copy(head_ref, g_ref.at[:, pl.ds(local, HALO * FRAME)], head_sem)
    fetch_head.start()
    loads[2].start()
    loads[3].start()

    for i in range(2):
        h_ref[i * 128 : (i + 1) * 128, :] = recv_ref[pl.ds(24 + i, GROUP, stride=ROWS), :].T

    @pl.loop(0, NODES)
    def _(n):
        blocks = [recv_ref[pl.ds(a * NODES + n, GROUP, stride=ROWS), :].T for a in range(3)]
        planes = [b[:SHOTS] for b in blocks] + [jnp.concatenate([b[SHOTS:] for b in blocks], 0)]
        halo = pl.multiple_of(n * 32, 32)
        pieces = [
            (HALO, SHOTS, planes),
            (0, HALO, [h_ref[pl.ds(halo + 8 * a, HALO), :] for a in range(4)]),
            (HALO + SHOTS, HALO, [h_ref[pl.ds(halo + 8 * a + HALO, HALO), :] for a in range(4)]),
        ]
        for first, size, values in pieces:
            for j in range(2):
                re, im = values[2 * j], values[2 * j + 1]
                co = cos_ref[first : first + size, j * 128 : (j + 1) * 128]
                si = sin_ref[first : first + size, j * 128 : (j + 1) * 128]
                place = 2 * j * rows_ext + first * NODES + n
                c_ref[pl.ds(place, size, stride=NODES), :] = 2.0 * (re * co + im * si)
                c_ref[pl.ds(place + rows_ext, size, stride=NODES), :] = 2.0 * (im * co - re * si)

    step = 80
    parity = 1.0 - 2.0 * (lax.broadcasted_iota(jnp.int32, (step, 128), 1) & 1).astype(f32)

    @pl.loop(0, rows_frames // step)
    def _(i):
        base = pl.multiple_of(i * step, NODES)

        def shot(m, a):
            return c_ref[pl.ds(pl.multiple_of(a * rows_ext + base + (HALO - m) * NODES, NODES), step), :]

        parts = [
            (shot(0, 0) - shot(2, 0)) - parity * (shot(1, 1) - shot(3, 1)),
            (shot(0, 1) - shot(2, 1)) + parity * (shot(1, 0) - shot(3, 0)),
            (shot(0, 2) + shot(2, 2)) - parity * (shot(1, 2) + shot(3, 2)),
            (shot(0, 3) + shot(2, 3)) - parity * (shot(1, 3) + shot(3, 3)),
        ]
        for a in range(4):
            hi, lo = split(parts[a])
            lh_ref[pl.ds(base, step), ORDER[a] * 128 : (ORDER[a] + 1) * 128] = hi
            ll_ref[pl.ds(base, step), ORDER[a] * 128 : (ORDER[a] + 1) * 128] = lo

    @pl.loop(0, rows_ext // 64)
    def _(i):
        base = pl.multiple_of(i * 64, 64)
        target = pl.multiple_of(rows_frames + base, 32)
        for a in range(4):
            hi, lo = split(c_ref[pl.ds(pl.multiple_of(a * rows_ext + base, 64), 64), :])
            lh_ref[pl.ds(target, 64), ORDER[a] * 128 : (ORDER[a] + 1) * 128] = hi
            ll_ref[pl.ds(target, 64), ORDER[a] * 128 : (ORDER[a] + 1) * 128] = lo

    width = 256
    lane = lax.broadcasted_iota(jnp.int32, (NODES, width), 1)
    mirror = 127 - lax.broadcasted_iota(jnp.int32, (NODES, 128), 1)

    def reverse(x):
        tiles = [x[:, i : i + 128] for i in range(0, x.shape[1], 128)]
        return jnp.concatenate([jnp.take_along_axis(t, mirror, axis=1) for t in tiles[::-1]], 1)

    def pair(row, size, c):
        cols = pl.ds(pl.multiple_of(c * width, width), width)
        rows = pl.ds(row, size)
        return (
            product(lh_ref[rows, :256], ll_ref[rows, :256], fh_ref[0, :, cols], fl_ref[0, :, cols]),
            product(lh_ref[rows, 256:], ll_ref[rows, 256:], fh_ref[1, :, cols], fl_ref[1, :, cols]),
        )

    def columns(c):
        return pl.multiple_of(512 + c * width, width), pl.multiple_of(256 - c * width, width)

    loads[0].wait()
    loads[1].wait()
    half_ext = rows_ext // 2

    @pl.loop(0, 4)
    def _(i):
        m, c = i // 2, i % 2
        even, odd = pair(pl.multiple_of(rows_frames + m * half_ext, 16), half_ext, c)
        upper, lower = columns(c)
        for s in range(EXT // 2):
            rows = slice(s * NODES, (s + 1) * NODES)
            place = pl.ds(pl.multiple_of(m * half_ext + s * NODES, NODES), NODES)
            d = d_ref[m * (EXT // 2) + s]
            q_ref[place, pl.ds(upper, width)] = jnp.where(lane < d - upper, even[rows] + odd[rows], 0.0)
            q_ref[place, pl.ds(lower, width)] = jnp.where(lane < d - lower, reverse(even[rows] - odd[rows]), 0.0)

    fetch.wait()
    fetch_head.wait()
    half_frames = rows_frames // 2

    @pl.loop(0, 4)
    def _(i):
        m, c = i // 2, i % 2
        even, odd = pair(pl.multiple_of(m * half_frames, 16), half_frames, c)
        upper, lower = columns(c)
        for f in range(FRAMES // 2):
            rows = slice(f * NODES, (f + 1) * NODES)
            first = m * half_frames + f * NODES
            now = pl.ds(pl.multiple_of(first, NODES), NODES)
            ahead = pl.ds(pl.multiple_of(first + HALO * NODES, NODES), NODES)
            start = (m * (FRAMES // 2) + f) * FRAME
            for col, out in ((upper, even[rows] + odd[rows]), (lower, reverse(even[rows] - odd[rows]))):
                cols = pl.ds(col, width)
                place = pl.ds(pl.multiple_of(start + col, width), width)
                g_ref[:, place] = g_ref[:, place] - out + (q_ref[ahead, cols] - q_ref[now, cols])

    @pl.when(last_ref[0] > 0)
    def _():
        g_ref[:, local:] = jnp.zeros((NODES, HALO * FRAME), f32)

    store = pltpu.make_async_copy(g_ref.at[:, pl.ds(0, local)], mis_ref, out_sem)
    store.start()

    wide = lax.broadcasted_iota(jnp.int32, (NODES, FRAME), 1)

    def put(row, first, second):
        folded = []
        for x in (first, second):
            back = reverse(x[:, :512])
            folded.append(jnp.concatenate([x[:, 512:] + back, x[:, 512:] - back], 1))
        hi, lo = split(jnp.concatenate(folded, 0))
        mh_ref[pl.ds(row, 16), :] = hi
        ml_ref[pl.ds(row, 16), :] = lo

    @pl.loop(0, FRAMES // 4)
    def _(i):
        now = [g_ref[:, pl.ds(pl.multiple_of((i * 4 + f) * FRAME, FRAME), FRAME)] for f in range(4)]
        base = pl.multiple_of(i * 32, 32)
        for f in range(0, 4, 2):
            put(base + f * NODES, now[f], now[f + 1])

        @pl.when(i < SHOTS // 4)
        def _():
            target = pl.multiple_of(rows_frames + base, 32)
            diffs = []
            for f in range(4):
                later = g_ref[:, pl.ds(pl.multiple_of((i * 4 + f + HALO) * FRAME, FRAME), FRAME)]
                diffs.append(jnp.where(wide < d_ref[i * 4 + f + HALO], later - now[f], 0.0))
            for f in range(0, 4, 2):
                put(target + f * NODES, diffs[f], diffs[f + 1])

    loads[2].wait()
    loads[3].wait()
    total = rows_frames + rows_local
    half = total // 2

    @pl.loop(0, 2)
    def _(i):
        row = pl.multiple_of(i * half, 16)
        rows = pl.ds(row, half)
        for part in range(2):
            cols = slice(part * 512, (part + 1) * 512)
            out = product(mh_ref[rows, cols], ml_ref[rows, cols], ah_ref[part], al_ref[part])
            for k in range(2):
                place = pl.multiple_of((2 * k + part) * total + row, 16)
                sp_ref[pl.ds(place, half), :] = out[:, k * 128 : (k + 1) * 128]

    band = 48
    sign = 1.0 - 2.0 * (lax.broadcasted_iota(jnp.int32, (band, 128), 1) & 1).astype(f32)

    @pl.loop(0, rows_local // band)
    def _(i):
        base = pl.multiple_of(i * band, NODES)

        def frame(m, a):
            return sp_ref[pl.ds(pl.multiple_of(a * total + base + m * NODES, NODES), band), :]

        def edge(a):
            return sp_ref[pl.ds(pl.multiple_of(a * total + rows_frames + base, NODES), band), :]

        parts = [
            (frame(0, 0) - frame(2, 0)) + sign * (frame(1, 1) - frame(3, 1)) + edge(0),
            (frame(0, 1) - frame(2, 1)) - sign * (frame(1, 0) - frame(3, 0)) + edge(1),
            (frame(0, 2) + frame(2, 2)) - sign * (frame(1, 2) + frame(3, 2)) + edge(2),
            (frame(0, 3) + frame(2, 3)) - sign * (frame(1, 3) + frame(3, 3)) + edge(3),
        ]
        for a in range(4):
            w_ref[pl.ds(pl.multiple_of(a * rows_local + base, NODES), band), :] = parts[a]

    @pl.loop(0, NODES)
    def _(n):
        parts = [w_ref[pl.ds(a * rows_local + n, SHOTS, stride=NODES), :] for a in range(4)]
        outs = []
        for j in range(2):
            co = RELAX * cos_ref[HALO : HALO + SHOTS, j * 128 : (j + 1) * 128]
            si = RELAX * sin_ref[HALO : HALO + SHOTS, j * 128 : (j + 1) * 128]
            re, im = parts[2 * j], parts[2 * j + 1]
            outs += [re * co - im * si, im * co + re * si]
        for a in range(3):
            block = jnp.concatenate([outs[a], outs[3][32 * a : 32 * a + 32]], 0).T
            send_ref[pl.ds(a * NODES + n, GROUP, stride=24), :] = block

    send = pltpu.make_async_copy(send_ref, send_hbm, send_sem)
    send.start()
    store.wait()
    send.wait()


def signal(dither, last, recv, cos_t, sin_t, tables, head, gathers):
    vmem = pl.BlockSpec(memory_space=pltpu.VMEM)
    smem = pl.BlockSpec(memory_space=pltpu.SMEM)
    hbm = pl.BlockSpec(memory_space=pltpu.HBM)
    rows_ext, rows_frames, rows_local = EXT * NODES, FRAMES * NODES, SHOTS * NODES
    return pl.pallas_call(
        signal_kernel,
        in_specs=[smem, smem, vmem, vmem, vmem, hbm, hbm, hbm, hbm, hbm, hbm],
        out_specs=[hbm, hbm],
        out_shape=[
            jax.ShapeDtypeStruct((NODES, SHOTS * FRAME), f32),
            jax.ShapeDtypeStruct((GROUP * 24, 128), f32),
        ],
        scratch_shapes=[
            pltpu.VMEM((4 * rows_ext, 128), f32),
            pltpu.VMEM((NODES, FRAMES * FRAME), f32),
            pltpu.VMEM((rows_ext, FRAME), f32),
            pltpu.VMEM((256, 128), f32),
            pltpu.VMEM((rows_frames + rows_ext, 512), bf16),
            pltpu.VMEM((rows_frames + rows_ext, 512), bf16),
            pltpu.VMEM((rows_frames + rows_local, FRAME), bf16),
            pltpu.VMEM((rows_frames + rows_local, FRAME), bf16),
            pltpu.VMEM((4 * (rows_frames + rows_local), 128), f32),
            pltpu.VMEM((4 * rows_local, 128), f32),
            pltpu.VMEM((GROUP * 24, 128), f32),
            pltpu.VMEM((2, 256, 512), bf16),
            pltpu.VMEM((2, 256, 512), bf16),
            pltpu.VMEM((2, 512, 256), bf16),
            pltpu.VMEM((2, 512, 256), bf16),
            pltpu.SemaphoreType.DMA,
            pltpu.SemaphoreType.DMA,
            pltpu.SemaphoreType.DMA,
            pltpu.SemaphoreType.DMA,
            pltpu.SemaphoreType.DMA((4,)),
        ],
        compiler_params=pltpu.CompilerParams(vmem_limit_bytes=40 << 20),
        name="signal",
    )(dither, last, recv, cos_t, sin_t, *tables, head, gathers)


def rank_kernel(recv_ref, est_hbm, w_ref, out_hbm, ah_ref, al_ref, est_ref, out_ref, in_sem, out_sem):
    chunks = 4
    size = 256 // chunks
    loads = [
        pltpu.make_async_copy(
            est_hbm.at[:, pl.ds(i * size, size), :], est_ref.at[:, pl.ds(i * size, size), :], in_sem.at[i]
        )
        for i in range(chunks)
    ]
    for load in loads:
        load.start()
    lane = lax.broadcasted_iota(jnp.int32, (NODES, 128), 1)
    chunk = lane // 32

    def planes(p):
        rows = pl.ds(pl.multiple_of(p * NODES, NODES), NODES)
        values, extras = [], []
        for a in range(3):
            t = []
            for q in range(4):
                tile = recv_ref[pl.ds(pl.multiple_of((p * 4 + q) * 24 + a * NODES, NODES), NODES), :]
                t.append(pltpu.roll(tile, (96 * q) % 128, axis=1) if q else tile)
            values.append([
                jnp.where(lane < 96, t[0], t[1]),
                jnp.where(lane < 64, t[1], t[2]),
                jnp.where(lane < 32, t[2], t[3]),
            ])
            e = jnp.where(chunk == 0, t[3], jnp.where(chunk == 1, t[2], jnp.where(chunk == 2, t[1], t[0])))
            extras.append(pltpu.roll(e, 32 * (a + 1), axis=1) if a < 3 else e)
        values.append([])
        for i in range(3):
            x = extras[(4 * i) % 3]
            for k in range(1, 4):
                x = jnp.where(chunk == k, extras[(4 * i + k) % 3], x)
            values[3].append(x)
        return [
            [est_ref[a, rows, i * 128 : (i + 1) * 128] + values[a][i] for i in range(3)] for a in range(4)
        ]

    def unpack(p):
        upper, lower = planes(2 * p), planes(2 * p + 1)
        rows = pl.ds(pl.multiple_of(p * 16, 16), 16)
        for a in range(4):
            for i in range(3):
                hi, lo = split(jnp.concatenate([upper[a][i], lower[a][i]], 0))
                cols = slice((a % 2) * 384 + i * 128, (a % 2) * 384 + (i + 1) * 128)
                ah_ref[a // 2, rows, cols] = hi
                al_ref[a // 2, rows, cols] = lo

    for i in range(chunks):
        loads[i].wait()
        pl.loop(i * (16 // chunks), (i + 1) * (16 // chunks))(unpack)

    dot = functools.partial(jnp.dot, preferred_element_type=f32)
    lane_r = lax.broadcasted_iota(jnp.int32, (64, 128), 1)
    row_r = lax.broadcasted_iota(jnp.int32, (64, 128), 0)
    flip = jnp.where(lane_r < 64, 1.0, -1.0).astype(f32)
    diagonal = (lane_r == row_r) & (row_r < RANK)
    systems = []
    rights = []
    basis = []
    for j in range(2):
        yy = dot(ah_ref[j], w_ref[...])
        y = yy[:, :128] + yy[:, 128:] + dot(al_ref[j], w_ref[:, :128])
        basis.append(split(y))
        yt = y.T
        g = jnp.dot(yt, y, precision=highest, preferred_element_type=f32)
        g = g[:64] + flip * pltpu.roll(g[64:], 64, axis=1)
        trace = jnp.sum(jnp.where(diagonal, g, 0.0))
        g = jnp.where(diagonal, g + RIDGE * trace / RANK, g)
        eye = jnp.where(diagonal, 1.0, 0.0).astype(f32)
        systems.append([g[:RANK], eye[:RANK]])
        yh, yl = split(yt)
        c = dot(jnp.concatenate([yh, yl], 0), ah_ref[j])
        c = c[:128] + c[128:] + dot(yh, al_ref[j])
        rights.append(jnp.concatenate([c[:64, :384] + c[64:, 384:], c[:64, 384:] - c[64:, :384]], 0))

    neg = jnp.where(lax.broadcasted_iota(jnp.int32, (1, 128), 1) < 64, -1.0, 1.0).astype(f32)
    row_i = lax.broadcasted_iota(jnp.int32, (RANK, 128), 0)
    for k in range(RANK - 1):
        start = ((k + 1) // 8) * 8
        for j in range(2):
            g, w = systems[j]
            gk, wk = g[k : k + 1], w[k : k + 1]
            inv = 1.0 / gk[:, k : k + 1]
            gk, wk = gk * inv, wk * inv
            gs, ws = neg * pltpu.roll(gk, 64, axis=1), neg * pltpu.roll(wk, 64, axis=1)
            below = g[start:]
            live = row_i[start:] > k
            cr = jnp.where(live, below[:, k : k + 1], 0.0)
            ci = jnp.where(live, below[:, 64 + k : 65 + k], 0.0)
            low_g = below - (cr * gk + ci * gs)
            low_w = w[start:] - (cr * wk + ci * ws)
            if start:
                low_g = jnp.concatenate([g[:start], low_g], 0)
                low_w = jnp.concatenate([w[:start], low_w], 0)
            systems[j] = [low_g, low_w]

    def two(left, right):
        lh, ll = split(left)
        rh, rl = split(right)
        return dot(jnp.concatenate([lh, ll], 1), jnp.concatenate([rh, rh], 0)) + dot(lh, rl)

    stores = []
    for j in range(2):
        g, w = systems[j]
        d = jnp.sum(jnp.where(diagonal[:RANK], g, 0.0), axis=1, keepdims=True)
        w = w * lax.rsqrt(d)
        w = jnp.concatenate([w, jnp.zeros((16, 128), f32)], 0)
        left = jnp.concatenate([flip * w, pltpu.roll(w, 64, axis=1)], 0)
        x = two(left.T, two(left, rights[j]))
        x = jnp.concatenate(
            [jnp.concatenate([x[:64], -x[64:]], 0), jnp.concatenate([x[64:], x[:64]], 0)], 1
        )
        xh, xl = split(x)
        yh, yl = basis[j]
        low = dot(jnp.concatenate([yh, yl], 1), jnp.concatenate([xh, xh], 0)) + dot(yh, xl)
        out_ref[2 * j] = low[:, :384]
        out_ref[2 * j + 1] = low[:, 384:]
        stores.append(
            pltpu.make_async_copy(out_ref.at[pl.ds(2 * j, 2)], out_hbm.at[pl.ds(2 * j, 2)], out_sem.at[j])
        )
        stores[-1].start()
    for store in stores:
        store.wait()


def rank_reduce(recv, est, w):
    vmem = pl.BlockSpec(memory_space=pltpu.VMEM)
    hbm = pl.BlockSpec(memory_space=pltpu.HBM)
    return pl.pallas_call(
        rank_kernel,
        in_specs=[vmem, hbm, vmem],
        out_specs=hbm,
        out_shape=jax.ShapeDtypeStruct((4, 256, 384), f32),
        scratch_shapes=[
            pltpu.VMEM((2, 256, 768), bf16),
            pltpu.VMEM((2, 256, 768), bf16),
            pltpu.VMEM((4, 256, 384), f32),
            pltpu.VMEM((4, 256, 384), f32),
            pltpu.SemaphoreType.DMA((4,)),
            pltpu.SemaphoreType.DMA((2,)),
        ],
        compiler_params=pltpu.CompilerParams(vmem_limit_bytes=20 << 20),
        name="rank",
    )(recv, est, w)


def table(rows_first):
    shape = (2, 256, FRAME // 2) if rows_first else (2, FRAME // 2, 256)
    part = lax.broadcasted_iota(jnp.int32, shape, 0)
    row = lax.broadcasted_iota(jnp.int32, shape, 1 if rows_first else 2)
    time = lax.broadcasted_iota(jnp.int32, shape, 2 if rows_first else 1)
    k = 2 * (row % 128) + row // 128 + 1
    phase = (k * (2 * time + 1) + part * (SPAN // 2)) % (2 * SPAN)
    value = jnp.cos(math.pi / SPAN * phase.astype(f32)) / math.sqrt(SPAN)
    hi = lax.reduce_precision(value, 8, 7)
    return hi.astype(bf16), (value - hi).astype(bf16)


def shards(receiver_gathers, fourier_estimate, random_projector, release_sample):
    q = lax.axis_index("freq")
    est = fourier_estimate.reshape(4, 32, NODES, 4 * SHOTS)
    send = pack(est).reshape(GROUP, ROWS // 2, 2, 128)
    recv = lax.all_to_all(send, ("node", "freq"), split_axis=0, concat_axis=0, tiled=True)

    up = [(0, 1), (1, 2), (2, 3)]
    down = [(1, 0), (2, 1), (3, 2)]
    head = lax.ppermute(receiver_gathers[:, : HALO * FRAME], "freq", down)
    release_before = lax.ppermute(release_sample[SHOTS - HALO :], "freq", up)
    release_after = lax.ppermute(release_sample[:HALO], "freq", down)
    dither = jnp.concatenate([release_before, release_sample, release_after]) % FRAME
    src = lax.iota(jnp.int32, 256)
    k = 2 * (src % 128) + src // 128 + 1
    angle = math.pi / SPAN * (k[None, :] * (2 * dither - FRAME + 1)[:, None] % (2 * SPAN)).astype(f32)
    cos_t, sin_t = jnp.cos(angle), jnp.sin(angle)
    tables = table(True) + table(False)
    last = (q == 3).astype(jnp.int32).reshape(1)
    misfit, back = signal(dither, last, recv.reshape(GROUP * ROWS, 128), cos_t, sin_t, tables, head, receiver_gathers)

    arrived = lax.all_to_all(
        back.reshape(GROUP, 24, 128), ("node", "freq"), split_axis=0, concat_axis=0, tiled=True
    )
    omega = jnp.pad(random_projector, ((0, 0), (0, 16)))
    zero = jnp.zeros_like(omega)
    w = jnp.concatenate([jnp.concatenate([omega, zero], 1), jnp.concatenate([zero, omega], 1)], 0)
    hi = lax.reduce_precision(w, 8, 7)
    w = jnp.concatenate([hi.astype(bf16), (w - hi).astype(bf16)], 1)
    low = rank_reduce(arrived.reshape(GROUP * 24, 128), fourier_estimate.reshape(4, 256, 384), w)
    return low.reshape(2, 2, 256, 384), misfit


def solution(mesh):
    return jax.shard_map(
        shards,
        mesh=mesh,
        in_specs=(P("node", "freq"), P(("node", "freq"), None, None, None), P(), P("freq")),
        out_specs=(P(("node", "freq"), None, None, None), P("node", "freq")),
        check_vma=False,
    )
```

time: 139 us -> 115 us (0.83)
  Pallas kernels: 55.7 us -> 39.4 us
  other arithmetic: 21.7 us -> 11.5 us
  local copies, waits for them, and re-layouts: 4.44 us -> 6.86 us
    pallas_call x2, Pallas kernels: 51.4 us -> 32.4 us  [the longest x1 18.4 us: signal(): pl.pallas_call(signal_kernel, in_specs=[smem, smem, vmem, vmem, vmem, hbm...]
    convert_element_type x2, other arithmetic: 19.2 us -> 10 us  [table(): return (hi.astype(bf16), (value - hi).astype(bf16))]
    pallas_call x1, Pallas kernels: 4.29 us -> 7.02 us  [pack(): pl.pallas_call(pack_kernel, grid=(32 // step,), in_specs=[pl.BlockSpec((4...]
    unnamed x13 -> x15, local copies, waits for them, and re-layouts: 2.63 us -> 5.2 us
  transfers between devices with their start and end apart: 5 -> 5, of which waited for: 3 -> 3; matrix products, arithmetic and copies ran while one was open for 17% -> 12% of each run, Pallas kernels for 3% -> 0%
where the time goes in v1:
time: 115 us; the launch traced here: 114 us
  Pallas kernels  39.4 us (34%)
  waiting for transfers between devices  31.9 us (28%)
  starting transfers between devices  23.4 us (20%)
  other arithmetic  11.5 us (10%)
  local copies, waits for them, and re-layouts  6.86 us (6%)
    all_to_all x1, waiting for transfers between devices, shards(): lax.all_to_all(back.reshape(GROUP, 24, 128), ('node', 'freq'), split_axis...  23.7 us
    pallas_call x1, Pallas kernels, signal(): pl.pallas_call(signal_kernel, in_specs=[smem, smem, vmem, vmem, vmem, hbm...  18.4 us
    pallas_call x1, Pallas kernels, rank_reduce(): pl.pallas_call(rank_kernel, in_specs=[vmem, hbm, vmem], out_specs=hbm, ou...  13.9 us
    all_to_all x1, starting transfers between devices, shards(): lax.all_to_all(send, ('node', 'freq'), split_axis=0, concat_axis=0, tiled...  11.5 us
    convert_element_type x2, other arithmetic, table(): return (hi.astype(bf16), (value - hi).astype(bf16))  10 us
    pallas_call x1, Pallas kernels, pack(): pl.pallas_call(pack_kernel, grid=(32 // step,), in_specs=[pl.BlockSpec((4...  7.02 us
    all_to_all x1, starting transfers between devices, shards(): lax.all_to_all(back.reshape(GROUP, 24, 128), ('node', 'freq'), split_axis...  6.11 us
    unnamed x15, local copies, waits for them, and re-layouts  5.2 us
  transfers between devices with their start and end apart: 5, of which 3 were waited for; matrix products, arithmetic and copies ran while one was open for 12% of the time, Pallas kernels for 0%

profile of v1, /device:TPU:1, one launch (start us, length us, event | category | flops | bytes accessed | tf_op | source)
XLA Modules:
  0.0 114.0 jit_solution(17258493772899241633)
XLA Ops:
  0.6 7.0 %pack.1 = f32[3328,128]{1,0:T(8,128)} custom-call(f32[4,32,8,384]{3,2,1,0:T(8,128)} %bitcast.9), custom_call_target="tpu_custom_call" | custom-call | tf_op jit(solution)/shard_map/pack/pallas_call | solution.py:87
  7.7 0.0 copy-start.6
  7.7 11.5 %all-to-all-start = ((f32[128,13,2,128]{3,2,1,0:T(2,128)}), f32[128,13,2,128]{3,2,1,0:T(2,128)S(1)}, u32[]{:S(2)}, u32[]{:S(2)}) async-start(f32[128,13,2,128]{3,2,1,0:T(2,128)} %bitcast.13), calls=%async_computation | async-start | bytes 3407872 | tf_op jit(solution)/shard_map/all_to_all | solution.py:532
  19.1 0.0 copy-done.6
  19.2 0.1 fusion.26
  19.2 3.2 %collective-permute-start = (s32[4]{0:T(128)S(1)}, s32[4]{0:T(128)S(1)}, u32[]{:S(2)}, u32[]{:S(2)}) collective-permute-start(s32[4]{0:T(128)S(1)} %get-tuple-element.16), channel_id=1, source_target_pairs={{0,1},{1,2},{2,3},{4,5},{5,6},{6,7},{8,9},{9,10},{10,11},{12,13},{... | collective-permute-start | bytes 56 | tf_op jit(solution)/shard_map/ppermute | solution.py:537
  22.5 1.3 %collective-permute-start.1 = (s32[4]{0:T(128)S(1)}, s32[4]{0:T(128)S(1)}, u32[]{:S(2)}, u32[]{:S(2)}) collective-permute-start(s32[4]{0:T(128)S(1)} %get-tuple-element.17), channel_id=1, source_target_pairs={{1,0},{2,1},{3,2},{5,4},{6,5},{7,6},{9,8},{10,9},{11,10},{13,12},{... | collective-permute-start | bytes 56 | tf_op jit(solution)/shard_map/ppermute | solution.py:538
  23.8 1.6 %slice.11 = f32[8,4096]{1,0:T(8,128)} slice(f32[8,98304]{1,0:T(8,128)} %gath_ref.1), slice={[0:8], [0:4096]} | slice | bytes 262144 | tf_op jit(solution)/shard_map/slice | solution.py:536
  25.4 1.3 %collective-permute-start.2 = (f32[8,4096]{1,0:T(8,128)}, f32[8,4096]{1,0:T(8,128)}, u32[]{:S(2)}, u32[]{:S(2)}) collective-permute-start(f32[8,4096]{1,0:T(8,128)} %slice.11), channel_id=1, source_target_pairs={{1,0},{2,1},{3,2},{5,4},{6,5},{7,6},{9,8},{10,9},{11,10},{13,12},{... | collective-permute-start | bytes 393224 | tf_op jit(solution)/shard_map/ppermute | solution.py:536
  26.7 4.6 %fusion.1 = (bf16[2,512,256]{2,1,0:T(8,128)(2,1)S(1)}, bf16[2,512,256]{2,1,0:T(8,128)(2,1)S(1)}) fusion(s32[2]{0:T(128)S(1)} %iota_multiply_fusion, s32[512]{0:T(512)S(1)} %multiply_add_fusion, s32[256]{0:T(256)S(1)} %get-tuple-element.18, s32[256]{0:T(256)S(1)} %get-tuple-element.23, pred[256]{0:T(512)(128)(4,1)S(1)} %get-tuple-element.20, ...), kind=kLoop, calls=%fused_computation.11 | loop fusion | flops 6553600 | bytes 1055240 | tf_op jit(solution)/shard_map/convert_element_type | solution.py:525
  31.3 5.4 %fusion = (bf16[2,256,512]{2,1,0:T(8,128)(2,1)S(1)}, bf16[2,256,512]{2,1,0:T(8,128)(2,1)}) fusion(s32[2]{0:T(128)S(1)} %iota_multiply_fusion, s32[512]{0:T(512)S(1)} %multiply_add_fusion, s32[256]{0:T(256)S(1)} %get-tuple-element.18, s32[256]{0:T(256)S(1)} %get-tuple-element.23, pred[256]{0:T(512)(128)(4,1)S(1)} %get-tuple-element.20, ...), kind=kLoop, calls=%fused_computation.10 | loop fusion | flops 6553600 | bytes 1055240 | tf_op jit(solution)/shard_map/convert_element_type | solution.py:525
  36.7 0.0 collective-permute-done
  36.7 0.0 collective-permute-done.1
  36.7 0.1 multiply_add_fusion.1
  36.8 0.5 fusion.16
  37.3 4.4 %collective-permute-done.2.head_ref = f32[8,4096]{1,0:T(8,128)} collective-permute-done((f32[8,4096]{1,0:T(8,128)}, f32[8,4096]{1,0:T(8,128)}, u32[]{:S(2)}, u32[]{:S(2)}) %collective-permute-start.2) | collective-permute-done | bytes 131104 | tf_op jit(solution)/shard_map/ppermute | solution.py:536
  41.7 3.8 %all-to-all-done = f32[128,13,2,128]{3,2,1,0:T(2,128)S(1)} async-done(((f32[128,13,2,128]{3,2,1,0:T(2,128)}), f32[128,13,2,128]{3,2,1,0:T(2,128)S(1)}, u32[]{:S(2)}, u32[]{:S(2)}) %all-to-all-start) | async-done | bytes 1703968 | tf_op jit(solution)/shard_map/all_to_all | solution.py:532
  45.5 0.0 copy-start.1
  45.5 1.9 %copy-done.1 = f32[8,98304]{1,0:T(8,128)S(1)} copy-done((f32[8,98304]{1,0:T(8,128)S(1)}, f32[8,98304]{1,0:T(8,128)}, u32[]{:S(2)}) %copy-start.1) | copy-done | bytes 3145752
  47.4 0.0 copy-start.2
  47.4 1.0 copy-done.2
  48.4 18.4 %signal.1 = (f32[8,98304]{1,0:T(8,128)}, f32[3072,128]{1,0:T(8,128)S(1)}) custom-call(s32[104]{0:T(128)S(1)} %get-tuple-element.7.d_ref, s32[1]{0:T(128)} %bitcast.last_ref, f32[3328,128]{1,0:T(8,128)S(1)} %bitcast.8, f32[104,256]{1,0:T(8,128)S(1)} %get-tuple-element.15.cos_ref, f32[104,256]{1,0:T(8,128)S(1)} %get-tuple-element.14.sin_ref, ...), custom_call_target="tpu_custom_call" | custom-call | tf_op jit(solution)/shard_map/signal/pallas_call | solution.py:333
  66.9 0.0 copy-start.3
  66.9 1.1 copy-done.3
  68.0 0.0 copy-start.5
  68.0 6.1 %all-to-all-start.1 = ((f32[128,24,128]{2,1,0:T(8,128)}), f32[128,24,128]{2,1,0:T(8,128)S(1)}, u32[]{:S(2)}, u32[]{:S(2)}) async-start(f32[128,24,128]{2,1,0:T(8,128)} %bitcast.12), calls=%async_computation.1 | async-start | bytes 3145728 | tf_op jit(solution)/shard_map/all_to_all | solution.py:548
  74.2 0.0 copy-done.5
  74.2 0.0 copy-start
  74.2 0.1 copy.6
  74.3 0.1 reduce-precision_convert_fusion.2
  74.5 0.8 pad_maximum_fusion.w_ref
  75.3 23.7 %all-to-all-done.1 = f32[128,24,128]{2,1,0:T(8,128)S(1)} async-done(((f32[128,24,128]{2,1,0:T(8,128)}), f32[128,24,128]{2,1,0:T(8,128)S(1)}, u32[]{:S(2)}, u32[]{:S(2)}) %all-to-all-start.1) | async-done | bytes 1572896 | tf_op jit(solution)/shard_map/all_to_all | solution.py:548
  99.0 0.0 copy-done
  99.0 0.0 copy-start.4
  99.0 1.0 copy-done.4
  100.0 13.9 %rank.1 = f32[4,256,384]{2,1,0:T(8,128)} custom-call(f32[3072,128]{1,0:T(8,128)S(1)} %bitcast.11, f32[4,256,384]{2,1,0:T(8,128)S(1)} %bitcast.10, bf16[768,256]{1,0:T(8,128)(2,1)S(1)} %copy-done.4), custom_call_target="tpu_custom_call" | custom-call | tf_op jit(solution)/shard_map/rank/pallas_call | solution.py:498
  (7 shorter events, 0.0 us)
Async XLA Ops:
  7.7 11.5 %copy-start.6 = (s32[96]{0:T(128)S(1)}, s32[96]{0:T(128)}, u32[]{:S(2)}) copy-start(s32[96]{0:T(128)} %param.7) | copy-start | bytes 1156
  7.7 37.8 %all-to-all-start = ((f32[128,13,2,128]{3,2,1,0:T(2,128)}), f32[128,13,2,128]{3,2,1,0:T(2,128)S(1)}, u32[]{:S(2)}, u32[]{:S(2)}) async-start(f32[128,13,2,128]{3,2,1,0:T(2,128)} %bitcast.13), calls=%async_computation | async-start | bytes 3407872 | tf_op jit(solution)/shard_map/all_to_all | solution.py:532
  19.2 17.5 %collective-permute-start = (s32[4]{0:T(128)S(1)}, s32[4]{0:T(128)S(1)}, u32[]{:S(2)}, u32[]{:S(2)}) collective-permute-start(s32[4]{0:T(128)S(1)} %get-tuple-element.16), channel_id=1, source_target_pairs={{0,1},{1,2},{2,3},{4,5},{5,6},{6,7},{8,9},{9,10},{10,11},{12,13},{... | collective-permute-start | bytes 56 | tf_op jit(solution)/shard_map/ppermute | solution.py:537
  22.5 14.2 %collective-permute-start.1 = (s32[4]{0:T(128)S(1)}, s32[4]{0:T(128)S(1)}, u32[]{:S(2)}, u32[]{:S(2)}) collective-permute-start(s32[4]{0:T(128)S(1)} %get-tuple-element.17), channel_id=1, source_target_pairs={{1,0},{2,1},{3,2},{5,4},{6,5},{7,6},{9,8},{10,9},{11,10},{13,12},{... | collective-permute-start | bytes 56 | tf_op jit(solution)/shard_map/ppermute | solution.py:538
  25.4 16.3 %collective-permute-start.2 = (f32[8,4096]{1,0:T(8,128)}, f32[8,4096]{1,0:T(8,128)}, u32[]{:S(2)}, u32[]{:S(2)}) collective-permute-start(f32[8,4096]{1,0:T(8,128)} %slice.11), channel_id=1, source_target_pairs={{1,0},{2,1},{3,2},{5,4},{6,5},{7,6},{9,8},{10,9},{11,10},{13,12},{... | collective-permute-start | bytes 393224 | tf_op jit(solution)/shard_map/ppermute | solution.py:536
  45.5 1.9 %copy-start.1 = (f32[8,98304]{1,0:T(8,128)S(1)}, f32[8,98304]{1,0:T(8,128)}, u32[]{:S(2)}) copy-start(f32[8,98304]{1,0:T(8,128)} %gath_ref.1) | copy-start | bytes 9437188
  47.4 1.0 copy-start.2
  66.9 1.1 %copy-start.3 = (f32[3072,128]{1,0:T(8,128)}, f32[3072,128]{1,0:T(8,128)S(1)}, u32[]{:S(2)}) copy-start(f32[3072,128]{1,0:T(8,128)S(1)} %get-tuple-element.4) | copy-start | bytes 4718596
  68.0 6.1 %copy-start.5 = (f32[384,48]{0,1:T(8,128)S(1)}, f32[384,48]{0,1:T(8,128)}, u32[]{:S(2)}) copy-start(f32[384,48]{0,1:T(8,128)} %param.6) | copy-start | bytes 221188
  68.0 30.9 %all-to-all-start.1 = ((f32[128,24,128]{2,1,0:T(8,128)}), f32[128,24,128]{2,1,0:T(8,128)S(1)}, u32[]{:S(2)}, u32[]{:S(2)}) async-start(f32[128,24,128]{2,1,0:T(8,128)} %bitcast.12), calls=%async_computation.1 | async-start | bytes 3145728 | tf_op jit(solution)/shard_map/all_to_all | solution.py:548
  74.2 24.8 %copy-start = (f32[2,2,256,384]{3,2,1,0:T(8,128)S(1)}, f32[2,2,256,384]{3,2,1,0:T(8,128)}, u32[]{:S(2)}) copy-start(f32[2,2,256,384]{3,2,1,0:T(8,128)} %param.5) | copy-start | bytes 4718596
  99.0 1.0 copy-start.4

commit v2 on v1

--- a/solution.py
+++ b/solution.py
@@ -27,14 +27,35 @@
 bf16 = jnp.bfloat16
 
 
+def keep(x):
+    return pltpu.with_memory_space_constraint(x, pltpu.HBM)
+
+
+def aligned(x, n):
+    return x if isinstance(x, int) else pl.multiple_of(x, n)
+
+
 def split(x):
     hi = x.astype(bf16)
     lo = (x - hi.astype(f32)).astype(bf16)
     return hi, lo
 
 
-def pack_kernel(x_ref, o_ref):
-    count = x_ref.shape[1]
+def pack_kernel(x_hbm, o_hbm, x_ref, o_ref, in_sem, out_sem):
+    chunks = 4
+    count = 32 // chunks
+    size = count * 4 * ROWS
+
+    def load(i):
+        part = pl.ds(i * count, count)
+        return pltpu.make_async_copy(x_hbm.at[:, part], x_ref.at[:, part], in_sem.at[i])
+
+    def store(i):
+        part = pl.ds(aligned(i * size, 8), size)
+        return pltpu.make_async_copy(o_ref.at[part], o_hbm.at[part], out_sem.at[i])
+
+    for i in range(chunks):
+        load(i).start()
     lane = lax.broadcasted_iota(jnp.int32, (NODES, 128), 1)
     node = lax.broadcasted_iota(jnp.int32, (NODES, 128), 0)
     slot = lane // 32
@@ -43,8 +64,7 @@
     def turn(v, by):
         return pltpu.roll(v, by % 128, axis=1) if by % 128 else v
 
-    @pl.loop(0, count)
-    def _(p):
+    def one(p, start):
         x = [[x_ref[a, p, :, i * 128 : (i + 1) * 128] for i in range(3)] for a in range(4)]
         edges = jnp.zeros((NODES, 128), f32)
         for k in range(3):
@@ -62,7 +82,7 @@
         spreads = [spread(k) for k in range(3)]
         zero = jnp.zeros((NODES, 128), f32)
         for q in range(4):
-            base = (p * 4 + q) * ROWS
+            base = start + q * ROWS
             for a in range(3):
                 if q == 0:
                     main = x[a][0]
@@ -81,18 +101,32 @@
             o_ref[pl.ds(base + 24, 1), :] = halo[3:4]
             o_ref[pl.ds(base + 25, 1), :] = halo[7:8]
 
+    @pl.loop(0, chunks)
+    def _(step):
+        load(step).wait()
+        for p in range(count):
+            one(step * count + p, aligned(step * size, 8) + p * 4 * ROWS)
+        store(step).start()
+
+    for i in range(chunks):
+        store(i).wait()
+
 
 def pack(x):
-    step = 8
+    hbm = pl.BlockSpec(memory_space=pltpu.HBM)
     return pl.pallas_call(
         pack_kernel,
-        grid=(32 // step,),
-        in_specs=[pl.BlockSpec((4, step, NODES, 4 * SHOTS), lambda i: (0, i, 0, 0))],
-        out_specs=pl.BlockSpec((step * 4 * ROWS, 128), lambda i: (i, 0)),
-        out_shape=jax.ShapeDtypeStruct((GROUP * ROWS, 128), f32),
-        compiler_params=pltpu.CompilerParams(vmem_limit_bytes=56 << 20),
+        in_specs=[hbm],
+        out_specs=hbm,
+        out_shape=pltpu.HBM((GROUP * ROWS, 128), f32),
+        scratch_shapes=[
+            pltpu.VMEM((4, 32, NODES, 4 * SHOTS), f32),
+            pltpu.VMEM((GROUP * ROWS, 128), f32),
+            pltpu.SemaphoreType.DMA((4,)),
+            pltpu.SemaphoreType.DMA((4,)),
+        ],
         name="pack",
-    )(x)
+    )(keep(x))
 
 
 def product(hi, lo, th, tl):
@@ -121,7 +155,7 @@
     loads[1].start()
     fetch = pltpu.make_async_copy(gath_ref, g_ref.at[:, pl.ds(0, local)], in_sem)
     fetch.start()
-    fetch_head = pltpu.make_async_copy(head_ref, g_ref.at[:, pl.ds(local, HALO * FRAME)], head_sem)
+    fetch_head = pltpu.make_async_copy(head_ref.at[:, pl.ds(0, HALO * FRAME)], g_ref.at[:, pl.ds(local, HALO * FRAME)], head_sem)
     fetch_head.start()
     loads[2].start()
     loads[3].start()
@@ -133,7 +167,7 @@
     def _(n):
         blocks = [recv_ref[pl.ds(a * NODES + n, GROUP, stride=ROWS), :].T for a in range(3)]
         planes = [b[:SHOTS] for b in blocks] + [jnp.concatenate([b[SHOTS:] for b in blocks], 0)]
-        halo = pl.multiple_of(n * 32, 32)
+        halo = aligned(n * 32, 32)
         pieces = [
             (HALO, SHOTS, planes),
             (0, HALO, [h_ref[pl.ds(halo + 8 * a, HALO), :] for a in range(4)]),
@@ -153,10 +187,10 @@
 
     @pl.loop(0, rows_frames // step)
     def _(i):
-        base = pl.multiple_of(i * step, NODES)
+        base = aligned(i * step, NODES)
 
         def shot(m, a):
-            return c_ref[pl.ds(pl.multiple_of(a * rows_ext + base + (HALO - m) * NODES, NODES), step), :]
+            return c_ref[pl.ds(aligned(a * rows_ext + base + (HALO - m) * NODES, NODES), step), :]
 
         parts = [
             (shot(0, 0) - shot(2, 0)) - parity * (shot(1, 1) - shot(3, 1)),
@@ -171,10 +205,10 @@
 
     @pl.loop(0, rows_ext // 64)
     def _(i):
-        base = pl.multiple_of(i * 64, 64)
-        target = pl.multiple_of(rows_frames + base, 32)
+        base = aligned(i * 64, 64)
+        target = aligned(rows_frames + base, 32)
         for a in range(4):
-            hi, lo = split(c_ref[pl.ds(pl.multiple_of(a * rows_ext + base, 64), 64), :])
+            hi, lo = split(c_ref[pl.ds(aligned(a * rows_ext + base, 64), 64), :])
             lh_ref[pl.ds(target, 64), ORDER[a] * 128 : (ORDER[a] + 1) * 128] = hi
             ll_ref[pl.ds(target, 64), ORDER[a] * 128 : (ORDER[a] + 1) * 128] = lo
 
@@ -187,7 +221,7 @@
         return jnp.concatenate([jnp.take_along_axis(t, mirror, axis=1) for t in tiles[::-1]], 1)
 
     def pair(row, size, c):
-        cols = pl.ds(pl.multiple_of(c * width, width), width)
+        cols = pl.ds(aligned(c * width, width), width)
         rows = pl.ds(row, size)
         return (
             product(lh_ref[rows, :256], ll_ref[rows, :256], fh_ref[0, :, cols], fl_ref[0, :, cols]),
@@ -195,20 +229,19 @@
         )
 
     def columns(c):
-        return pl.multiple_of(512 + c * width, width), pl.multiple_of(256 - c * width, width)
+        return aligned(512 + c * width, width), aligned(256 - c * width, width)
 
     loads[0].wait()
     loads[1].wait()
     half_ext = rows_ext // 2
 
-    @pl.loop(0, 4)
-    def _(i):
+    for i in range(4):
         m, c = i // 2, i % 2
-        even, odd = pair(pl.multiple_of(rows_frames + m * half_ext, 16), half_ext, c)
+        even, odd = pair(aligned(rows_frames + m * half_ext, 16), half_ext, c)
         upper, lower = columns(c)
         for s in range(EXT // 2):
             rows = slice(s * NODES, (s + 1) * NODES)
-            place = pl.ds(pl.multiple_of(m * half_ext + s * NODES, NODES), NODES)
+            place = pl.ds(aligned(m * half_ext + s * NODES, NODES), NODES)
             d = d_ref[m * (EXT // 2) + s]
             q_ref[place, pl.ds(upper, width)] = jnp.where(lane < d - upper, even[rows] + odd[rows], 0.0)
             q_ref[place, pl.ds(lower, width)] = jnp.where(lane < d - lower, reverse(even[rows] - odd[rows]), 0.0)
@@ -217,25 +250,20 @@
     fetch_head.wait()
     half_frames = rows_frames // 2
 
-    @pl.loop(0, 4)
-    def _(i):
+    for i in range(4):
         m, c = i // 2, i % 2
-        even, odd = pair(pl.multiple_of(m * half_frames, 16), half_frames, c)
+        even, odd = pair(aligned(m * half_frames, 16), half_frames, c)
         upper, lower = columns(c)
         for f in range(FRAMES // 2):
             rows = slice(f * NODES, (f + 1) * NODES)
             first = m * half_frames + f * NODES
-            now = pl.ds(pl.multiple_of(first, NODES), NODES)
-            ahead = pl.ds(pl.multiple_of(first + HALO * NODES, NODES), NODES)
+            now = pl.ds(aligned(first, NODES), NODES)
+            ahead = pl.ds(aligned(first + HALO * NODES, NODES), NODES)
             start = (m * (FRAMES // 2) + f) * FRAME
             for col, out in ((upper, even[rows] + odd[rows]), (lower, reverse(even[rows] - odd[rows]))):
                 cols = pl.ds(col, width)
-                place = pl.ds(pl.multiple_of(start + col, width), width)
+                place = pl.ds(aligned(start + col, width), width)
                 g_ref[:, place] = g_ref[:, place] - out + (q_ref[ahead, cols] - q_ref[now, cols])
-
-    @pl.when(last_ref[0] > 0)
-    def _():
-        g_ref[:, local:] = jnp.zeros((NODES, HALO * FRAME), f32)
 
     store = pltpu.make_async_copy(g_ref.at[:, pl.ds(0, local)], mis_ref, out_sem)
     store.start()
@@ -251,51 +279,51 @@
         mh_ref[pl.ds(row, 16), :] = hi
         ml_ref[pl.ds(row, 16), :] = lo
 
-    @pl.loop(0, FRAMES // 4)
-    def _(i):
-        now = [g_ref[:, pl.ds(pl.multiple_of((i * 4 + f) * FRAME, FRAME), FRAME)] for f in range(4)]
-        base = pl.multiple_of(i * 32, 32)
-        for f in range(0, 4, 2):
-            put(base + f * NODES, now[f], now[f + 1])
-
-        @pl.when(i < SHOTS // 4)
-        def _():
-            target = pl.multiple_of(rows_frames + base, 32)
-            diffs = []
-            for f in range(4):
-                later = g_ref[:, pl.ds(pl.multiple_of((i * 4 + f + HALO) * FRAME, FRAME), FRAME)]
-                diffs.append(jnp.where(wide < d_ref[i * 4 + f + HALO], later - now[f], 0.0))
-            for f in range(0, 4, 2):
-                put(target + f * NODES, diffs[f], diffs[f + 1])
-
-    loads[2].wait()
-    loads[3].wait()
+    def frame_at(f):
+        return g_ref[:, pl.ds(aligned(f * FRAME, FRAME), FRAME)]
+
+    inside = last_ref[0] == 0
+
+    def residual(f):
+        x = frame_at(f)
+        return x if f < SHOTS else jnp.where(inside, x, 0.0)
+
     total = rows_frames + rows_local
     half = total // 2
 
-    @pl.loop(0, 2)
-    def _(i):
-        row = pl.multiple_of(i * half, 16)
-        rows = pl.ds(row, half)
+    def adjoint(i):
+        rows = slice(i * half, (i + 1) * half)
         for part in range(2):
             cols = slice(part * 512, (part + 1) * 512)
             out = product(mh_ref[rows, cols], ml_ref[rows, cols], ah_ref[part], al_ref[part])
             for k in range(2):
-                place = pl.multiple_of((2 * k + part) * total + row, 16)
-                sp_ref[pl.ds(place, half), :] = out[:, k * 128 : (k + 1) * 128]
+                place = (2 * k + part) * total + i * half
+                sp_ref[place : place + half, :] = out[:, k * 128 : (k + 1) * 128]
+
+    def edge_of(f):
+        return jnp.where(wide < d_ref[f + HALO], residual(f + HALO) - residual(f), 0.0)
+
+    for f in range(0, FRAMES, 2):
+        put(f * NODES, residual(f), residual(f + 1))
+    loads[2].wait()
+    loads[3].wait()
+    adjoint(0)
+    for f in range(0, SHOTS, 2):
+        put(rows_frames + f * NODES, edge_of(f), edge_of(f + 1))
+    adjoint(1)
 
     band = 48
     sign = 1.0 - 2.0 * (lax.broadcasted_iota(jnp.int32, (band, 128), 1) & 1).astype(f32)
 
     @pl.loop(0, rows_local // band)
     def _(i):
-        base = pl.multiple_of(i * band, NODES)
+        base = aligned(i * band, NODES)
 
         def frame(m, a):
-            return sp_ref[pl.ds(pl.multiple_of(a * total + base + m * NODES, NODES), band), :]
+            return sp_ref[pl.ds(aligned(a * total + base + m * NODES, NODES), band), :]
 
         def edge(a):
-            return sp_ref[pl.ds(pl.multiple_of(a * total + rows_frames + base, NODES), band), :]
+            return sp_ref[pl.ds(aligned(a * total + rows_frames + base, NODES), band), :]
 
         parts = [
             (frame(0, 0) - frame(2, 0)) + sign * (frame(1, 1) - frame(3, 1)) + edge(0),
@@ -304,10 +332,9 @@
             (frame(0, 3) + frame(2, 3)) - sign * (frame(1, 3) + frame(3, 3)) + edge(3),
         ]
         for a in range(4):
-            w_ref[pl.ds(pl.multiple_of(a * rows_local + base, NODES), band), :] = parts[a]
-
-    @pl.loop(0, NODES)
-    def _(n):
+            w_ref[pl.ds(aligned(a * rows_local + base, NODES), band), :] = parts[a]
+
+    def emit(n):
         parts = [w_ref[pl.ds(a * rows_local + n, SHOTS, stride=NODES), :] for a in range(4)]
         outs = []
         for j in range(2):
@@ -319,6 +346,11 @@
             block = jnp.concatenate([outs[a], outs[3][32 * a : 32 * a + 32]], 0).T
             send_ref[pl.ds(a * NODES + n, GROUP, stride=24), :] = block
 
+    @pl.loop(0, NODES // 2)
+    def _(n):
+        emit(2 * n)
+        emit(2 * n + 1)
+
     send = pltpu.make_async_copy(send_ref, send_hbm, send_sem)
     send.start()
     store.wait()
@@ -335,8 +367,8 @@
         in_specs=[smem, smem, vmem, vmem, vmem, hbm, hbm, hbm, hbm, hbm, hbm],
         out_specs=[hbm, hbm],
         out_shape=[
-            jax.ShapeDtypeStruct((NODES, SHOTS * FRAME), f32),
-            jax.ShapeDtypeStruct((GROUP * 24, 128), f32),
+            pltpu.HBM((NODES, SHOTS * FRAME), f32),
+            pltpu.HBM((GROUP * 24, 128), f32),
         ],
         scratch_shapes=[
             pltpu.VMEM((4 * rows_ext, 128), f32),
@@ -362,10 +394,12 @@
         ],
         compiler_params=pltpu.CompilerParams(vmem_limit_bytes=40 << 20),
         name="signal",
-    )(dither, last, recv, cos_t, sin_t, *tables, head, gathers)
-
-
-def rank_kernel(recv_ref, est_hbm, w_ref, out_hbm, ah_ref, al_ref, est_ref, out_ref, in_sem, out_sem):
+    )(dither, last, recv, cos_t, sin_t, *[keep(t) for t in tables], keep(head), keep(gathers))
+
+
+def rank_kernel(
+    recv_ref, est_hbm, w_hbm, out_hbm, ah_ref, al_ref, est_ref, out_ref, w_ref, in_sem, out_sem, w_sem
+):
     chunks = 4
     size = 256 // chunks
     loads = [
@@ -376,16 +410,18 @@
     ]
     for load in loads:
         load.start()
+    load_w = pltpu.make_async_copy(w_hbm, w_ref, w_sem)
+    load_w.start()
     lane = lax.broadcasted_iota(jnp.int32, (NODES, 128), 1)
     chunk = lane // 32
 
     def planes(p):
-        rows = pl.ds(pl.multiple_of(p * NODES, NODES), NODES)
+        rows = pl.ds(aligned(p * NODES, NODES), NODES)
         values, extras = [], []
         for a in range(3):
             t = []
             for q in range(4):
-                tile = recv_ref[pl.ds(pl.multiple_of((p * 4 + q) * 24 + a * NODES, NODES), NODES), :]
+                tile = recv_ref[pl.ds(aligned((p * 4 + q) * 24 + a * NODES, NODES), NODES), :]
                 t.append(pltpu.roll(tile, (96 * q) % 128, axis=1) if q else tile)
             values.append([
                 jnp.where(lane < 96, t[0], t[1]),
@@ -406,7 +442,7 @@
 
     def unpack(p):
         upper, lower = planes(2 * p), planes(2 * p + 1)
-        rows = pl.ds(pl.multiple_of(p * 16, 16), 16)
+        rows = pl.ds(aligned(p * 16, 16), 16)
         for a in range(4):
             for i in range(3):
                 hi, lo = split(jnp.concatenate([upper[a][i], lower[a][i]], 0))
@@ -416,7 +452,13 @@
 
     for i in range(chunks):
         loads[i].wait()
-        pl.loop(i * (16 // chunks), (i + 1) * (16 // chunks))(unpack)
+
+        @pl.loop(0, 2)
+        def _(p, i=i):
+            unpack(i * 4 + p * 2)
+            unpack(i * 4 + p * 2 + 1)
+
+    load_w.wait()
 
     dot = functools.partial(jnp.dot, preferred_element_type=f32)
     lane_r = lax.broadcasted_iota(jnp.int32, (64, 128), 1)
@@ -442,26 +484,50 @@
         c = c[:128] + c[128:] + dot(yh, al_ref[j])
         rights.append(jnp.concatenate([c[:64, :384] + c[64:, 384:], c[:64, 384:] - c[64:, :384]], 0))
 
-    neg = jnp.where(lax.broadcasted_iota(jnp.int32, (1, 128), 1) < 64, -1.0, 1.0).astype(f32)
-    row_i = lax.broadcasted_iota(jnp.int32, (RANK, 128), 0)
-    for k in range(RANK - 1):
-        start = ((k + 1) // 8) * 8
-        for j in range(2):
-            g, w = systems[j]
-            gk, wk = g[k : k + 1], w[k : k + 1]
-            inv = 1.0 / gk[:, k : k + 1]
-            gk, wk = gk * inv, wk * inv
-            gs, ws = neg * pltpu.roll(gk, 64, axis=1), neg * pltpu.roll(wk, 64, axis=1)
-            below = g[start:]
-            live = row_i[start:] > k
-            cr = jnp.where(live, below[:, k : k + 1], 0.0)
-            ci = jnp.where(live, below[:, 64 + k : 65 + k], 0.0)
-            low_g = below - (cr * gk + ci * gs)
-            low_w = w[start:] - (cr * wk + ci * ws)
-            if start:
-                low_g = jnp.concatenate([g[:start], low_g], 0)
-                low_w = jnp.concatenate([w[:start], low_w], 0)
-            systems[j] = [low_g, low_w]
+    neg = jnp.where(lax.broadcasted_iota(jnp.int32, (NODES, 128), 1) < 64, -1.0, 1.0).astype(f32)
+    row_i = lax.broadcasted_iota(jnp.int32, (NODES, 128), 0)
+    groups = RANK // NODES
+    state = [
+        ([g[i * NODES : (i + 1) * NODES] for i in range(groups)], [w[i * NODES : (i + 1) * NODES] for i in range(groups)])
+        for g, w in systems
+    ]
+
+    def row(x, k):
+        return jnp.broadcast_to(x[k % NODES : k % NODES + 1], (NODES, 128))
+
+    def column(x, k):
+        return jnp.broadcast_to(x[:, k : k + 1], (NODES, 128))
+
+    def turned(x):
+        return neg * pltpu.roll(x, 64, axis=1)
+
+    for k in range(0, RANK, 2):
+        top = k // NODES
+        for gs, ws in state:
+            gt, wt = turned(gs[top]), turned(ws[top])
+            cols = [[column(gs[i], c) for c in (k, 64 + k, k + 1, 65 + k)] for i in range(top, groups)]
+            a = row(cols[0][0], k)
+            br, bi = row(cols[0][2], k), row(cols[0][3], k)
+            d = row(cols[0][2], k + 1)
+            ia = 1.0 / a
+            lr, li = br * ia, -bi * ia
+            second = 1.0 / (d - (br * br + bi * bi) * ia)
+            g0, g0i, w0, w0i = row(gs[top], k), row(gt, k), row(ws[top], k), row(wt, k)
+            g1 = row(gs[top], k + 1) - (lr * g0 + li * g0i)
+            g1i = row(gt, k + 1) - (lr * g0i - li * g0)
+            w1 = row(ws[top], k + 1) - (lr * w0 + li * w0i)
+            w1i = row(wt, k + 1) - (lr * w0i - li * w0)
+            for i in range(top, groups):
+                c0r, c0i, c1r, c1i = cols[i - top]
+                f0r, f0i = c0r * ia, c0i * ia
+                f1r = (c1r - (f0r * br - f0i * bi)) * second
+                f1i = (c1i - (f0r * bi + f0i * br)) * second
+                if i == top:
+                    f0r, f0i = jnp.where(row_i > k % NODES, f0r, 0.0), jnp.where(row_i > k % NODES, f0i, 0.0)
+                    f1r, f1i = jnp.where(row_i > k % NODES + 1, f1r, 0.0), jnp.where(row_i > k % NODES + 1, f1i, 0.0)
+                gs[i] = gs[i] - ((f0r * g0 + f0i * g0i) + (f1r * g1 + f1i * g1i))
+                ws[i] = ws[i] - ((f0r * w0 + f0i * w0i) + (f1r * w1 + f1i * w1i))
+    systems = [[jnp.concatenate(gs, 0), jnp.concatenate(ws, 0)] for gs, ws in state]
 
     def two(left, right):
         lh, ll = split(left)
@@ -497,30 +563,49 @@
     hbm = pl.BlockSpec(memory_space=pltpu.HBM)
     return pl.pallas_call(
         rank_kernel,
-        in_specs=[vmem, hbm, vmem],
+        in_specs=[vmem, hbm, hbm],
         out_specs=hbm,
-        out_shape=jax.ShapeDtypeStruct((4, 256, 384), f32),
+        out_shape=pltpu.HBM((4, 256, 384), f32),
         scratch_shapes=[
             pltpu.VMEM((2, 256, 768), bf16),
             pltpu.VMEM((2, 256, 768), bf16),
             pltpu.VMEM((4, 256, 384), f32),
             pltpu.VMEM((4, 256, 384), f32),
+            pltpu.VMEM((768, 256), bf16),
             pltpu.SemaphoreType.DMA((4,)),
             pltpu.SemaphoreType.DMA((2,)),
+            pltpu.SemaphoreType.DMA,
         ],
         compiler_params=pltpu.CompilerParams(vmem_limit_bytes=20 << 20),
         name="rank",
-    )(recv, est, w)
+    )(recv, keep(est), keep(w))
 
 
 def table(rows_first):
-    shape = (2, 256, FRAME // 2) if rows_first else (2, FRAME // 2, 256)
-    part = lax.broadcasted_iota(jnp.int32, shape, 0)
-    row = lax.broadcasted_iota(jnp.int32, shape, 1 if rows_first else 2)
-    time = lax.broadcasted_iota(jnp.int32, shape, 2 if rows_first else 1)
+    half = FRAME // 2
+    fine = 128 if rows_first else 64
+    row = lax.iota(jnp.int32, 256)
     k = 2 * (row % 128) + row // 128 + 1
-    phase = (k * (2 * time + 1) + part * (SPAN // 2)) % (2 * SPAN)
-    value = jnp.cos(math.pi / SPAN * phase.astype(f32)) / math.sqrt(SPAN)
+    near = 2 * lax.iota(jnp.int32, fine) + 1
+    far = 2 * fine * lax.iota(jnp.int32, half // fine)
+    if rows_first:
+        phases = k[:, None] * near[None, :], k[:, None] * far[None, :]
+    else:
+        phases = near[:, None] * k[None, :], far[:, None] * k[None, :]
+    angles = [math.pi / SPAN * (p % (2 * SPAN)).astype(f32) for p in phases]
+    scale = 1.0 / math.sqrt(SPAN)
+    cn, sn = jnp.cos(angles[0]) * scale, jnp.sin(angles[0]) * scale
+    cf, sf = jnp.cos(angles[1]), jnp.sin(angles[1])
+    cn, sn, cf, sf = lax.optimization_barrier((cn, sn, cf, sf))
+    if rows_first:
+        pieces = [
+            (cn * cf[:, i : i + 1] - sn * sf[:, i : i + 1], -(sn * cf[:, i : i + 1] + cn * sf[:, i : i + 1]))
+            for i in range(half // fine)
+        ]
+        value = jnp.stack([jnp.concatenate([p[j] for p in pieces], 1) for j in range(2)])
+    else:
+        cn, sn, cf, sf = cn[None], sn[None], cf[:, None], sf[:, None]
+        value = jnp.stack([cn * cf - sn * sf, -(sn * cf + cn * sf)]).reshape(2, half, 256)
     hi = lax.reduce_precision(value, 8, 7)
     return hi.astype(bf16), (value - hi).astype(bf16)
 
@@ -533,9 +618,12 @@
 
     up = [(0, 1), (1, 2), (2, 3)]
     down = [(1, 0), (2, 1), (3, 2)]
-    head = lax.ppermute(receiver_gathers[:, : HALO * FRAME], "freq", down)
+    starts = jnp.broadcast_to(jnp.pad(release_sample[:HALO].astype(f32), (0, 124))[None], (NODES, 128))
+    head = lax.ppermute(
+        jnp.concatenate([receiver_gathers[:, : HALO * FRAME], starts], 1), "freq", down
+    )
     release_before = lax.ppermute(release_sample[SHOTS - HALO :], "freq", up)
-    release_after = lax.ppermute(release_sample[:HALO], "freq", down)
+    release_after = head[0, HALO * FRAME : HALO * FRAME + HALO].astype(jnp.int32)
     dither = jnp.concatenate([release_before, release_sample, release_after]) % FRAME
     src = lax.iota(jnp.int32, 256)
     k = 2 * (src % 128) + src // 128 + 1

time: 115 us -> 102 us (0.89)
  waiting for transfers between devices: 31.9 us -> 45.4 us
  Pallas kernels: 39.4 us -> 26.3 us
  local copies, waits for them, and re-layouts: 6.86 us -> 1.08 us
  other arithmetic: 11.5 us -> 6.39 us
  starting transfers between devices: 23.4 us -> 21.2 us
    all_to_all x1, waiting for transfers between devices: 3.82 us -> 21.6 us  [shards(): lax.all_to_all(send, ('node', 'freq'), split_axis=0, concat_axis=0, tiled...]
    convert_element_type x2, other arithmetic: 10 us -> 2.3 us  [table(): return (hi.astype(bf16), (value - hi).astype(bf16))]
    pallas_call x1, Pallas kernels: 18.4 us -> 11.1 us  [signal(): pl.pallas_call(signal_kernel, in_specs=[smem, smem, vmem, vmem, vmem, hbm...]
    pallas_call x2, Pallas kernels: 20.9 us -> 15.2 us  [the longest x1 10.3 us: rank_reduce(): pl.pallas_call(rank_kernel, in_specs=[vmem, hbm, hbm], out_specs=hbm, out...]
    unnamed x15 -> x7, local copies, waits for them, and re-layouts: 5.2 us -> 0.14 us
    ppermute x2 -> x1, waiting for transfers between devices: 4.37 us -> 0.01 us  [shards(): lax.ppermute(jnp.concatenate([receiver_gathers[:, :HALO * FRAME], starts]...]
    all_to_all x1, starting transfers between devices: 6.11 us -> 3.9 us  [shards(): lax.all_to_all(back.reshape(GROUP, 24, 128), ('node', 'freq'), split_axis...]
    ppermute x1, starting transfers between devices: 3.25 us -> 4.65 us  [shards(): release_before = lax.ppermute(release_sample[SHOTS - HALO:], 'freq', up)]
  transfers between devices with their start and end apart: 5 -> 4, of which waited for: 3 -> 2; matrix products, arithmetic and copies ran while one was open for 12% -> 6% of each run, Pallas kernels for 0% -> 5%
where the time goes in v2:
time: 102 us; the launch traced here: 101 us
  waiting for transfers between devices  45.4 us (45%)
  Pallas kernels  26.3 us (26%)
  starting transfers between devices  21.2 us (21%)
  other arithmetic  6.39 us (6%)
  local copies, waits for them, and re-layouts  1.08 us (1%)
  between operations  1.02 us (1%)
    all_to_all x1, waiting for transfers between devices, shards(): lax.all_to_all(back.reshape(GROUP, 24, 128), ('node', 'freq'), split_axis...  23.9 us
    all_to_all x1, waiting for transfers between devices, shards(): lax.all_to_all(send, ('node', 'freq'), split_axis=0, concat_axis=0, tiled...  21.6 us
    all_to_all x1, starting transfers between devices, shards(): lax.all_to_all(send, ('node', 'freq'), split_axis=0, concat_axis=0, tiled...  11.4 us
    pallas_call x1, Pallas kernels, signal(): pl.pallas_call(signal_kernel, in_specs=[smem, smem, vmem, vmem, vmem, hbm...  11.1 us
    pallas_call x1, Pallas kernels, rank_reduce(): pl.pallas_call(rank_kernel, in_specs=[vmem, hbm, hbm], out_specs=hbm, out...  10.3 us
    pallas_call x1, Pallas kernels, pack(): pl.pallas_call(pack_kernel, in_specs=[hbm], out_specs=hbm, out_shape=pltp...  4.91 us
    ppermute x1, starting transfers between devices, shards(): release_before = lax.ppermute(release_sample[SHOTS - HALO:], 'freq', up)  4.65 us
    all_to_all x1, starting transfers between devices, shards(): lax.all_to_all(back.reshape(GROUP, 24, 128), ('node', 'freq'), split_axis...  3.9 us
  transfers between devices with their start and end apart: 4, of which 2 were waited for; matrix products, arithmetic and copies ran while one was open for 6% of the time, Pallas kernels for 5%

profile of v2, /device:TPU:1, one launch (start us, length us, event | category | flops | bytes accessed | tf_op | source)
XLA Modules:
  0.0 101.4 jit_solution(2256753677103938113)
XLA Ops:
  0.6 0.8 fusion.33
  1.4 0.9 slice.45
  2.4 1.3 %collective-permute-start.1 = (f32[8,4224]{1,0:T(8,128)S(1)}, f32[8,4224]{1,0:T(8,128)S(1)}, u32[]{:S(2)}, u32[]{:S(2)}) collective-permute-start(f32[8,4224]{1,0:T(8,128)S(1)} %pad_maximum_fusion.3), channel_id=1, source_target_pairs={{1,0},{2,1},{3,2},{5,4},{6,5},{7,6},{9,8},{10,9},{11,10},{13,12},{... | collective-permute-start | bytes 405512 | tf_op jit(solution)/shard_map/ppermute | solution.py:622
  3.7 4.6 %collective-permute-start = (s32[4]{0:T(128)S(1)}, s32[4]{0:T(128)S(1)}, u32[]{:S(2)}, u32[]{:S(2)}) collective-permute-start(s32[4]{0:T(128)S(1)} %get-tuple-element.64), channel_id=1, source_target_pairs={{0,1},{1,2},{2,3},{4,5},{5,6},{6,7},{8,9},{9,10},{10,11},{12,13},{... | collective-permute-start | bytes 56 | tf_op jit(solution)/shard_map/ppermute | solution.py:625
  8.3 4.9 %pack.1 = f32[3328,128]{1,0:T(8,128)} custom-call(f32[4,32,8,384]{3,2,1,0:T(8,128)} %bitcast.27), custom_call_target="tpu_custom_call" | custom-call | tf_op jit(solution)/shard_map/pack/pallas_call | solution.py:117
  13.2 11.4 %all-to-all-start = ((f32[128,13,2,128]{3,2,1,0:T(2,128)}), f32[128,13,2,128]{3,2,1,0:T(2,128)S(1)}, u32[]{:S(2)}, u32[]{:S(2)}) async-start(f32[128,13,2,128]{3,2,1,0:T(2,128)} %bitcast.26), calls=%async_computation | async-start | bytes 3407872 | tf_op jit(solution)/shard_map/all_to_all | solution.py:617
  24.7 0.6 sine_multiply_fusion
  25.3 0.1 fusion.22
  25.4 0.3 sine_multiply_fusion.1
  25.8 0.1 fusion.20
  25.9 0.3 multiply_subtract_fusion.4
  26.4 1.2 %fusion = (bf16[2,256,512]{2,1,0:T(8,128)(2,1)}, bf16[2,256,512]{2,1,0:T(8,128)(2,1)}) fusion(f32[1,256,512]{2,1,0:T(8,128)S(1)} %maximum_bitcast_fusion.1, f32[1,256,512]{2,1,0:T(8,128)S(1)} %maximum_bitcast_fusion), kind=kLoop, calls=%fused_computation.4 | loop fusion | flops 1310720 | bytes 2097152 | tf_op jit(solution)/shard_map/convert_element_type | solution.py:610
  27.5 0.0 copy-start.2
  27.5 0.1 multiply_subtract_fusion
  27.7 1.1 %fusion.1 = (bf16[2,512,256]{2,1,0:T(8,128)(2,1)}, bf16[2,512,256]{2,1,0:T(8,128)(2,1)}) fusion(f32[1,512,256]{2,1,0:T(8,128)S(1)} %bitcast.30, f32[1,512,256]{2,1,0:T(8,128)S(1)} %bitcast.29), kind=kLoop, calls=%fused_computation.5 | loop fusion | flops 1310720 | bytes 2097152 | tf_op jit(solution)/shard_map/convert_element_type | solution.py:610
  28.8 0.0 collective-permute-done.1.head_ref
  28.8 0.0 copy-start
  28.8 0.0 collective-permute-done
  28.8 0.0 copy-done.2
  28.9 0.1 multiply_add_fusion.2
  28.9 0.5 fusion.12
  29.4 21.6 %all-to-all-done = f32[128,13,2,128]{3,2,1,0:T(2,128)S(1)} async-done(((f32[128,13,2,128]{3,2,1,0:T(2,128)}), f32[128,13,2,128]{3,2,1,0:T(2,128)S(1)}, u32[]{:S(2)}, u32[]{:S(2)}) %all-to-all-start) | async-done | bytes 1703968 | tf_op jit(solution)/shard_map/all_to_all | solution.py:617
  51.0 0.0 copy-done
  51.0 11.1 %signal.1 = (f32[8,98304]{1,0:T(8,128)}, f32[3072,128]{1,0:T(8,128)}) custom-call(s32[104]{0:T(128)S(1)} %get-tuple-element.23.d_ref, s32[1]{0:T(128)} %bitcast.1.last_ref, f32[3328,128]{1,0:T(8,128)S(1)} %bitcast.24, f32[104,256]{1,0:T(8,128)S(1)} %get-tuple-element.63.cos_ref, f32[104,256]{1,0:T(8,128)S(1)} %get-tuple-element.62.sin_ref, ...), custom_call_target="tpu_custom_call" | custom-call | tf_op jit(solution)/shard_map/signal/pallas_call | solution.py:365
  62.1 0.0 copy-start.1
  62.1 3.9 %all-to-all-start.1 = ((f32[128,24,128]{2,1,0:T(8,128)}), f32[128,24,128]{2,1,0:T(8,128)S(1)}, u32[]{:S(2)}, u32[]{:S(2)}) async-start(f32[128,24,128]{2,1,0:T(8,128)} %bitcast.31), calls=%async_computation.1 | async-start | bytes 3145728 | tf_op jit(solution)/shard_map/all_to_all | solution.py:636
  66.0 0.0 copy-done.1
  66.0 0.1 copy.7
  66.2 0.1 reduce-precision_convert_fusion.2
  66.3 0.8 pad_maximum_fusion.2.w_hbm
  67.1 23.9 %all-to-all-done.1 = f32[128,24,128]{2,1,0:T(8,128)S(1)} async-done(((f32[128,24,128]{2,1,0:T(8,128)}), f32[128,24,128]{2,1,0:T(8,128)S(1)}, u32[]{:S(2)}, u32[]{:S(2)}) %all-to-all-start.1) | async-done | bytes 1572896 | tf_op jit(solution)/shard_map/all_to_all | solution.py:636
  91.0 10.3 %rank.1 = f32[4,256,384]{2,1,0:T(8,128)} custom-call(f32[3072,128]{1,0:T(8,128)S(1)} %bitcast.25, f32[4,256,384]{2,1,0:T(8,128)} %bitcast.28, bf16[768,256]{1,0:T(8,128)(2,1)} %pad_maximum_fusion.2.w_hbm), custom_call_target="tpu_custom_call" | custom-call | tf_op jit(solution)/shard_map/rank/pallas_call | solution.py:564
  (12 shorter events, 0.2 us)
Async XLA Ops:
  2.4 26.4 %collective-permute-start.1 = (f32[8,4224]{1,0:T(8,128)S(1)}, f32[8,4224]{1,0:T(8,128)S(1)}, u32[]{:S(2)}, u32[]{:S(2)}) collective-permute-start(f32[8,4224]{1,0:T(8,128)S(1)} %pad_maximum_fusion.3), channel_id=1, source_target_pairs={{1,0},{2,1},{3,2},{5,4},{6,5},{7,6},{9,8},{10,9},{11,10},{13,12},{... | collective-permute-start | bytes 405512 | tf_op jit(solution)/shard_map/ppermute | solution.py:622
  3.7 25.2 %collective-permute-start = (s32[4]{0:T(128)S(1)}, s32[4]{0:T(128)S(1)}, u32[]{:S(2)}, u32[]{:S(2)}) collective-permute-start(s32[4]{0:T(128)S(1)} %get-tuple-element.64), channel_id=1, source_target_pairs={{0,1},{1,2},{2,3},{4,5},{5,6},{6,7},{8,9},{9,10},{10,11},{12,13},{... | collective-permute-start | bytes 56 | tf_op jit(solution)/shard_map/ppermute | solution.py:625
  13.2 37.8 %all-to-all-start = ((f32[128,13,2,128]{3,2,1,0:T(2,128)}), f32[128,13,2,128]{3,2,1,0:T(2,128)S(1)}, u32[]{:S(2)}, u32[]{:S(2)}) async-start(f32[128,13,2,128]{3,2,1,0:T(2,128)} %bitcast.26), calls=%async_computation | async-start | bytes 3407872 | tf_op jit(solution)/shard_map/all_to_all | solution.py:617
  27.5 1.3 %copy-start.2 = (s32[96]{0:T(128)S(1)}, s32[96]{0:T(128)}, u32[]{:S(2)}) copy-start(s32[96]{0:T(128)} %param.7) | copy-start | bytes 1156
  28.8 22.2 %copy-start = (f32[8,4224]{1,0:T(8,128)}, f32[8,4224]{1,0:T(8,128)S(1)}, u32[]{:S(2)}) copy-start(f32[8,4224]{1,0:T(8,128)S(1)} %collective-permute-done.1.head_ref) | copy-start | bytes 405508
  62.1 3.9 %copy-start.1 = (f32[384,48]{0,1:T(8,128)S(1)}, f32[384,48]{0,1:T(8,128)}, u32[]{:S(2)}) copy-start(f32[384,48]{0,1:T(8,128)} %param.6) | copy-start | bytes 221188
  62.1 28.9 %all-to-all-start.1 = ((f32[128,24,128]{2,1,0:T(8,128)}), f32[128,24,128]{2,1,0:T(8,128)S(1)}, u32[]{:S(2)}, u32[]{:S(2)}) async-start(f32[128,24,128]{2,1,0:T(8,128)} %bitcast.31), calls=%async_computation.1 | async-start | bytes 3145728 | tf_op jit(solution)/shard_map/all_to_all | solution.py:636

commit v3 on v2

--- a/solution.py
+++ b/solution.py
@@ -19,6 +19,7 @@
 FRAMES = SHOTS + HALO
 GROUP = 128
 ROWS = 26
+PACK_CHUNKS = 8
 ORDER = (0, 2, 1, 3)
 RELAX = 0.25
 RIDGE = 0.001
@@ -42,9 +43,14 @@
 
 
 def pack_kernel(x_hbm, o_hbm, x_ref, o_ref, in_sem, out_sem):
-    chunks = 4
+    chunks = PACK_CHUNKS
     count = 32 // chunks
     size = count * 4 * ROWS
+    lane = lax.broadcasted_iota(jnp.int32, (1, NODES, 128), 2)
+    node = lax.broadcasted_iota(jnp.int32, (1, NODES, 128), 1)
+    slot = lane // 32
+    own = slot == node % 4
+    shape = (count, NODES, 128)
 
     def load(i):
         part = pl.ds(i * count, count)
@@ -54,58 +60,59 @@
         part = pl.ds(aligned(i * size, 8), size)
         return pltpu.make_async_copy(o_ref.at[part], o_hbm.at[part], out_sem.at[i])
 
+    def pick(mask, x, y):
+        return jnp.where(jnp.broadcast_to(mask, shape), x, y)
+
+    def turn(v, by):
+        return pltpu.roll(v, by % 128, axis=2) if by % 128 else v
+
     for i in range(chunks):
         load(i).start()
-    lane = lax.broadcasted_iota(jnp.int32, (NODES, 128), 1)
-    node = lax.broadcasted_iota(jnp.int32, (NODES, 128), 0)
-    slot = lane // 32
-    own = slot == node % 4
-
-    def turn(v, by):
-        return pltpu.roll(v, by % 128, axis=1) if by % 128 else v
-
-    def one(p, start):
-        x = [[x_ref[a, p, :, i * 128 : (i + 1) * 128] for i in range(3)] for a in range(4)]
-        edges = jnp.zeros((NODES, 128), f32)
+
+    @pl.loop(0, chunks)
+    def _(step):
+        load(step).wait()
+        blocks = pl.ds(step * count, count)
+        x = [[x_ref[a, blocks, :, i * 128 : (i + 1) * 128] for i in range(3)] for a in range(4)]
+        zero = jnp.zeros(shape, f32)
+        edges = zero
         for k in range(3):
             for a in range(4):
                 moved = turn(x[a][k], 32 * k + 8 * a - (92 - 32 * k))
-                edges = jnp.where((slot == k) & ((lane // 8) % 4 == a), moved, edges)
+                edges = pick(lane // 8 == 4 * k + a, moved, edges)
         turned = [turn(edges, 32 * r) for r in range(4)]
 
         def spread(k):
             v = turned[(0 - k) % 4]
             for m in range(1, 4):
-                v = jnp.where(slot == m, turned[(m - k) % 4], v)
-            return jnp.where(own, v, 0.0)
+                v = pick(slot == m, turned[(m - k) % 4], v)
+            return pick(own, v, zero)
 
         spreads = [spread(k) for k in range(3)]
-        zero = jnp.zeros((NODES, 128), f32)
+
+        def put(row, value, size):
+            for p in range(count):
+                o_ref[pl.ds(aligned(step * chunk_rows, 8) + p * 4 * ROWS + row, size), :] = value[p]
+
+        chunk_rows = size
         for q in range(4):
-            base = start + q * ROWS
             for a in range(3):
                 if q == 0:
                     main = x[a][0]
                 elif q == 3:
                     main = turn(x[a][2], 96)
                 else:
-                    main = jnp.where(lane < 32 * q, turn(x[a][q - 1], 32 * q), turn(x[a][q], 32 * q))
+                    main = pick(lane < 32 * q, turn(x[a][q - 1], 32 * q), turn(x[a][q], 32 * q))
                 m = 3 * q + a
                 rest = turn(x[3][m // 4], 32 * (3 - m % 4))
-                o_ref[pl.ds(base + NODES * a, NODES), :] = jnp.where(lane < SHOTS, main, rest)
+                put(q * ROWS + NODES * a, pick(lane < SHOTS, main, rest), NODES)
             before = spreads[q - 1] if q > 0 else zero
             after = spreads[q] if q < 3 else zero
-            halo = jnp.where(lane % 8 < 4, before, after)
-            halo = halo + pltpu.roll(halo, 1, axis=0)
-            halo = halo + pltpu.roll(halo, 2, axis=0)
-            o_ref[pl.ds(base + 24, 1), :] = halo[3:4]
-            o_ref[pl.ds(base + 25, 1), :] = halo[7:8]
-
-    @pl.loop(0, chunks)
-    def _(step):
-        load(step).wait()
-        for p in range(count):
-            one(step * count + p, aligned(step * size, 8) + p * 4 * ROWS)
+            halo = pick(lane % 8 < 4, before, after)
+            halo = halo + pltpu.roll(halo, 1, axis=1)
+            halo = halo + pltpu.roll(halo, 2, axis=1)
+            put(q * ROWS + 24, halo[:, 3:4], 1)
+            put(q * ROWS + 25, halo[:, 7:8], 1)
         store(step).start()
 
     for i in range(chunks):
@@ -122,8 +129,8 @@
         scratch_shapes=[
             pltpu.VMEM((4, 32, NODES, 4 * SHOTS), f32),
             pltpu.VMEM((GROUP * ROWS, 128), f32),
-            pltpu.SemaphoreType.DMA((4,)),
-            pltpu.SemaphoreType.DMA((4,)),
+            pltpu.SemaphoreType.DMA((PACK_CHUNKS,)),
+            pltpu.SemaphoreType.DMA((PACK_CHUNKS,)),
         ],
         name="pack",
     )(keep(x))
@@ -163,8 +170,7 @@
     for i in range(2):
         h_ref[i * 128 : (i + 1) * 128, :] = recv_ref[pl.ds(24 + i, GROUP, stride=ROWS), :].T
 
-    @pl.loop(0, NODES)
-    def _(n):
+    for n in range(NODES):
         blocks = [recv_ref[pl.ds(a * NODES + n, GROUP, stride=ROWS), :].T for a in range(3)]
         planes = [b[:SHOTS] for b in blocks] + [jnp.concatenate([b[SHOTS:] for b in blocks], 0)]
         halo = aligned(n * 32, 32)
@@ -185,8 +191,7 @@
     step = 80
     parity = 1.0 - 2.0 * (lax.broadcasted_iota(jnp.int32, (step, 128), 1) & 1).astype(f32)
 
-    @pl.loop(0, rows_frames // step)
-    def _(i):
+    def build(i):
         base = aligned(i * step, NODES)
 
         def shot(m, a):
@@ -203,8 +208,7 @@
             lh_ref[pl.ds(base, step), ORDER[a] * 128 : (ORDER[a] + 1) * 128] = hi
             ll_ref[pl.ds(base, step), ORDER[a] * 128 : (ORDER[a] + 1) * 128] = lo
 
-    @pl.loop(0, rows_ext // 64)
-    def _(i):
+    for i in range(rows_ext // 64):
         base = aligned(i * 64, 64)
         target = aligned(rows_frames + base, 32)
         for a in range(4):
@@ -245,6 +249,9 @@
             d = d_ref[m * (EXT // 2) + s]
             q_ref[place, pl.ds(upper, width)] = jnp.where(lane < d - upper, even[rows] + odd[rows], 0.0)
             q_ref[place, pl.ds(lower, width)] = jnp.where(lane < d - lower, reverse(even[rows] - odd[rows]), 0.0)
+
+    for i in range(rows_frames // step):
+        build(i)
 
     fetch.wait()
     fetch_head.wait()
@@ -315,8 +322,7 @@
     band = 48
     sign = 1.0 - 2.0 * (lax.broadcasted_iota(jnp.int32, (band, 128), 1) & 1).astype(f32)
 
-    @pl.loop(0, rows_local // band)
-    def _(i):
+    for i in range(rows_local // band):
         base = aligned(i * band, NODES)
 
         def frame(m, a):
@@ -346,10 +352,8 @@
             block = jnp.concatenate([outs[a], outs[3][32 * a : 32 * a + 32]], 0).T
             send_ref[pl.ds(a * NODES + n, GROUP, stride=24), :] = block
 
-    @pl.loop(0, NODES // 2)
-    def _(n):
-        emit(2 * n)
-        emit(2 * n + 1)
+    for n in range(NODES):
+        emit(n)
 
     send = pltpu.make_async_copy(send_ref, send_hbm, send_sem)
     send.start()
@@ -397,19 +401,7 @@
     )(dither, last, recv, cos_t, sin_t, *[keep(t) for t in tables], keep(head), keep(gathers))
 
 
-def rank_kernel(
-    recv_ref, est_hbm, w_hbm, out_hbm, ah_ref, al_ref, est_ref, out_ref, w_ref, in_sem, out_sem, w_sem
-):
-    chunks = 4
-    size = 256 // chunks
-    loads = [
-        pltpu.make_async_copy(
-            est_hbm.at[:, pl.ds(i * size, size), :], est_ref.at[:, pl.ds(i * size, size), :], in_sem.at[i]
-        )
-        for i in range(chunks)
-    ]
-    for load in loads:
-        load.start()
+def rank_kernel(recv_ref, est_ref, w_hbm, out_hbm, ah_ref, al_ref, out_ref, w_ref, out_sem, w_sem):
     load_w = pltpu.make_async_copy(w_hbm, w_ref, w_sem)
     load_w.start()
     lane = lax.broadcasted_iota(jnp.int32, (NODES, 128), 1)
@@ -450,13 +442,10 @@
                 ah_ref[a // 2, rows, cols] = hi
                 al_ref[a // 2, rows, cols] = lo
 
-    for i in range(chunks):
-        loads[i].wait()
-
-        @pl.loop(0, 2)
-        def _(p, i=i):
-            unpack(i * 4 + p * 2)
-            unpack(i * 4 + p * 2 + 1)
+    @pl.loop(0, 4)
+    def _(p):
+        for i in range(4):
+            unpack(4 * p + i)
 
     load_w.wait()
 
@@ -498,6 +487,9 @@
     def column(x, k):
         return jnp.broadcast_to(x[:, k : k + 1], (NODES, 128))
 
+    def gathered(x, k):
+        return jnp.take_along_axis(x, jnp.full((NODES, 128), k, jnp.int32), axis=1)
+
     def turned(x):
         return neg * pltpu.roll(x, 64, axis=1)
 
@@ -505,7 +497,10 @@
         top = k // NODES
         for gs, ws in state:
             gt, wt = turned(gs[top]), turned(ws[top])
-            cols = [[column(gs[i], c) for c in (k, 64 + k, k + 1, 65 + k)] for i in range(top, groups)]
+            cols = [
+                [(gathered if i == top else column)(gs[i], c) for c in (k, 64 + k, k + 1, 65 + k)]
+                for i in range(top, groups)
+            ]
             a = row(cols[0][0], k)
             br, bi = row(cols[0][2], k), row(cols[0][3], k)
             d = row(cols[0][2], k + 1)
@@ -563,22 +558,20 @@
     hbm = pl.BlockSpec(memory_space=pltpu.HBM)
     return pl.pallas_call(
         rank_kernel,
-        in_specs=[vmem, hbm, hbm],
+        in_specs=[vmem, vmem, hbm],
         out_specs=hbm,
         out_shape=pltpu.HBM((4, 256, 384), f32),
         scratch_shapes=[
             pltpu.VMEM((2, 256, 768), bf16),
             pltpu.VMEM((2, 256, 768), bf16),
             pltpu.VMEM((4, 256, 384), f32),
-            pltpu.VMEM((4, 256, 384), f32),
             pltpu.VMEM((768, 256), bf16),
-            pltpu.SemaphoreType.DMA((4,)),
             pltpu.SemaphoreType.DMA((2,)),
             pltpu.SemaphoreType.DMA,
         ],
         compiler_params=pltpu.CompilerParams(vmem_limit_bytes=20 << 20),
         name="rank",
-    )(recv, keep(est), keep(w))
+    )(recv, est, keep(w))
 
 
 def table(rows_first):

time: 102 us -> 96.8 us (0.949)
  Pallas kernels: 26.3 us -> 21.3 us
    pallas_call x1, Pallas kernels: 10.3 us -> 7.46 us  [rank_reduce(): pl.pallas_call(rank_kernel, in_specs=[vmem, vmem, hbm], out_specs=hbm, ou...]
    pallas_call x1, Pallas kernels: 11.1 us -> 9.81 us  [signal(): pl.pallas_call(signal_kernel, in_specs=[smem, smem, vmem, vmem, vmem, hbm...]
  transfers between devices with their start and end apart: 4 -> 4, of which waited for: 2 -> 2; matrix products, arithmetic and copies ran while one was open for 6% -> 6% of each run, Pallas kernels for 5% -> 4%
where the time goes in v3:
time: 96.8 us; the launch traced here: 96.4 us
  waiting for transfers between devices  45.4 us (47%)
  Pallas kernels  21.3 us (22%)
  starting transfers between devices  21.2 us (22%)
  other arithmetic  6.38 us (7%)
  local copies, waits for them, and re-layouts  1.08 us (1%)
  between operations  1.02 us (1%)
    all_to_all x1, waiting for transfers between devices, shards(): lax.all_to_all(back.reshape(GROUP, 24, 128), ('node', 'freq'), split_axis...  23.8 us
    all_to_all x1, waiting for transfers between devices, shards(): lax.all_to_all(send, ('node', 'freq'), split_axis=0, concat_axis=0, tiled...  21.6 us
    all_to_all x1, starting transfers between devices, shards(): lax.all_to_all(send, ('node', 'freq'), split_axis=0, concat_axis=0, tiled...  11.4 us
    pallas_call x1, Pallas kernels, signal(): pl.pallas_call(signal_kernel, in_specs=[smem, smem, vmem, vmem, vmem, hbm...  9.81 us
    pallas_call x1, Pallas kernels, rank_reduce(): pl.pallas_call(rank_kernel, in_specs=[vmem, vmem, hbm], out_specs=hbm, ou...  7.46 us
    ppermute x1, starting transfers between devices, shards(): release_before = lax.ppermute(release_sample[SHOTS - HALO:], 'freq', up)  4.65 us
    pallas_call x1, Pallas kernels, pack(): pl.pallas_call(pack_kernel, in_specs=[hbm], out_specs=hbm, out_shape=pltp...  4 us
    all_to_all x1, starting transfers between devices, shards(): lax.all_to_all(back.reshape(GROUP, 24, 128), ('node', 'freq'), split_axis...  3.9 us
  transfers between devices with their start and end apart: 4, of which 2 were waited for; matrix products, arithmetic and copies ran while one was open for 6% of the time, Pallas kernels for 4%

profile of v3, /device:TPU:1, one launch (start us, length us, event | category | flops | bytes accessed | tf_op | source)
XLA Modules:
  0.0 96.4 jit_solution(3791092682757927944)
XLA Ops:
  0.6 0.8 fusion.33
  1.4 0.9 slice.45
  2.4 1.3 %collective-permute-start.1 = (f32[8,4224]{1,0:T(8,128)S(1)}, f32[8,4224]{1,0:T(8,128)S(1)}, u32[]{:S(2)}, u32[]{:S(2)}) collective-permute-start(f32[8,4224]{1,0:T(8,128)S(1)} %pad_maximum_fusion.3), channel_id=1, source_target_pairs={{1,0},{2,1},{3,2},{5,4},{6,5},{7,6},{9,8},{10,9},{11,10},{13,12},{... | collective-permute-start | bytes 405512 | tf_op jit(solution)/shard_map/ppermute | solution.py:615
  3.7 4.6 %collective-permute-start = (s32[4]{0:T(128)S(1)}, s32[4]{0:T(128)S(1)}, u32[]{:S(2)}, u32[]{:S(2)}) collective-permute-start(s32[4]{0:T(128)S(1)} %get-tuple-element.64), channel_id=1, source_target_pairs={{0,1},{1,2},{2,3},{4,5},{5,6},{6,7},{8,9},{9,10},{10,11},{12,13},{... | collective-permute-start | bytes 56 | tf_op jit(solution)/shard_map/ppermute | solution.py:618
  8.3 4.0 %pack.1 = f32[3328,128]{1,0:T(8,128)} custom-call(f32[4,32,8,384]{3,2,1,0:T(8,128)} %bitcast.25), custom_call_target="tpu_custom_call" | custom-call | tf_op jit(solution)/shard_map/pack/pallas_call | solution.py:124
  12.3 11.4 %all-to-all-start = ((f32[128,13,2,128]{3,2,1,0:T(2,128)}), f32[128,13,2,128]{3,2,1,0:T(2,128)S(1)}, u32[]{:S(2)}, u32[]{:S(2)}) async-start(f32[128,13,2,128]{3,2,1,0:T(2,128)} %bitcast.28), calls=%async_computation | async-start | bytes 3407872 | tf_op jit(solution)/shard_map/all_to_all | solution.py:610
  23.8 0.6 sine_multiply_fusion
  24.4 0.1 fusion.22
  24.5 0.3 sine_multiply_fusion.1
  24.9 0.1 fusion.20
  25.0 0.3 multiply_subtract_fusion.4
  25.5 1.1 %fusion = (bf16[2,256,512]{2,1,0:T(8,128)(2,1)}, bf16[2,256,512]{2,1,0:T(8,128)(2,1)}) fusion(f32[1,256,512]{2,1,0:T(8,128)S(1)} %maximum_bitcast_fusion.1, f32[1,256,512]{2,1,0:T(8,128)S(1)} %maximum_bitcast_fusion), kind=kLoop, calls=%fused_computation.4 | loop fusion | flops 1310720 | bytes 2097152 | tf_op jit(solution)/shard_map/convert_element_type | solution.py:603
  26.6 0.0 copy-start.3
  26.6 0.1 multiply_subtract_fusion
  26.8 1.1 %fusion.1 = (bf16[2,512,256]{2,1,0:T(8,128)(2,1)}, bf16[2,512,256]{2,1,0:T(8,128)(2,1)}) fusion(f32[1,512,256]{2,1,0:T(8,128)S(1)} %bitcast.30, f32[1,512,256]{2,1,0:T(8,128)S(1)} %bitcast.29), kind=kLoop, calls=%fused_computation.5 | loop fusion | flops 1310720 | bytes 2097152 | tf_op jit(solution)/shard_map/convert_element_type | solution.py:603
  27.9 0.0 collective-permute-done.1.head_ref
  27.9 0.0 copy-start.1
  27.9 0.0 collective-permute-done
  27.9 0.0 copy-done.3
  27.9 0.1 multiply_add_fusion.2
  28.0 0.5 fusion.12
  28.5 21.6 %all-to-all-done = f32[128,13,2,128]{3,2,1,0:T(2,128)S(1)} async-done(((f32[128,13,2,128]{3,2,1,0:T(2,128)}), f32[128,13,2,128]{3,2,1,0:T(2,128)S(1)}, u32[]{:S(2)}, u32[]{:S(2)}) %all-to-all-start) | async-done | bytes 1703968 | tf_op jit(solution)/shard_map/all_to_all | solution.py:610
  50.1 0.0 copy-done.1
  50.1 9.8 %signal.1 = (f32[8,98304]{1,0:T(8,128)}, f32[3072,128]{1,0:T(8,128)}) custom-call(s32[104]{0:T(128)S(1)} %get-tuple-element.23.d_ref, s32[1]{0:T(128)} %bitcast.1.last_ref, f32[3328,128]{1,0:T(8,128)S(1)} %bitcast.24, f32[104,256]{1,0:T(8,128)S(1)} %get-tuple-element.63.cos_ref, f32[104,256]{1,0:T(8,128)S(1)} %get-tuple-element.62.sin_ref, ...), custom_call_target="tpu_custom_call" | custom-call | tf_op jit(solution)/shard_map/signal/pallas_call | solution.py:369
  59.9 0.0 copy-start.2
  59.9 3.9 %all-to-all-start.1 = ((f32[128,24,128]{2,1,0:T(8,128)}), f32[128,24,128]{2,1,0:T(8,128)S(1)}, u32[]{:S(2)}, u32[]{:S(2)}) async-start(f32[128,24,128]{2,1,0:T(8,128)} %bitcast.31), calls=%async_computation.1 | async-start | bytes 3145728 | tf_op jit(solution)/shard_map/all_to_all | solution.py:629
  63.9 0.0 copy-done.2
  63.9 0.0 copy-start
  63.9 0.1 copy.7
  64.0 0.1 reduce-precision_convert_fusion.2
  64.2 0.8 pad_maximum_fusion.2.w_hbm
  65.0 23.8 %all-to-all-done.1 = f32[128,24,128]{2,1,0:T(8,128)S(1)} async-done(((f32[128,24,128]{2,1,0:T(8,128)}), f32[128,24,128]{2,1,0:T(8,128)S(1)}, u32[]{:S(2)}, u32[]{:S(2)}) %all-to-all-start.1) | async-done | bytes 1572896 | tf_op jit(solution)/shard_map/all_to_all | solution.py:629
  88.8 0.0 copy-done
  88.8 7.5 %rank.1 = f32[4,256,384]{2,1,0:T(8,128)} custom-call(f32[3072,128]{1,0:T(8,128)S(1)} %bitcast.27, f32[4,256,384]{2,1,0:T(8,128)S(1)} %bitcast.26, bf16[768,256]{1,0:T(8,128)(2,1)} %pad_maximum_fusion.2.w_hbm), custom_call_target="tpu_custom_call" | custom-call | tf_op jit(solution)/shard_map/rank/pallas_call | solution.py:559
  (12 shorter events, 0.2 us)
Async XLA Ops:
  2.4 25.5 %collective-permute-start.1 = (f32[8,4224]{1,0:T(8,128)S(1)}, f32[8,4224]{1,0:T(8,128)S(1)}, u32[]{:S(2)}, u32[]{:S(2)}) collective-permute-start(f32[8,4224]{1,0:T(8,128)S(1)} %pad_maximum_fusion.3), channel_id=1, source_target_pairs={{1,0},{2,1},{3,2},{5,4},{6,5},{7,6},{9,8},{10,9},{11,10},{13,12},{... | collective-permute-start | bytes 405512 | tf_op jit(solution)/shard_map/ppermute | solution.py:615
  3.7 24.2 %collective-permute-start = (s32[4]{0:T(128)S(1)}, s32[4]{0:T(128)S(1)}, u32[]{:S(2)}, u32[]{:S(2)}) collective-permute-start(s32[4]{0:T(128)S(1)} %get-tuple-element.64), channel_id=1, source_target_pairs={{0,1},{1,2},{2,3},{4,5},{5,6},{6,7},{8,9},{9,10},{10,11},{12,13},{... | collective-permute-start | bytes 56 | tf_op jit(solution)/shard_map/ppermute | solution.py:618
  12.3 37.8 %all-to-all-start = ((f32[128,13,2,128]{3,2,1,0:T(2,128)}), f32[128,13,2,128]{3,2,1,0:T(2,128)S(1)}, u32[]{:S(2)}, u32[]{:S(2)}) async-start(f32[128,13,2,128]{3,2,1,0:T(2,128)} %bitcast.28), calls=%async_computation | async-start | bytes 3407872 | tf_op jit(solution)/shard_map/all_to_all | solution.py:610
  26.6 1.3 %copy-start.3 = (s32[96]{0:T(128)S(1)}, s32[96]{0:T(128)}, u32[]{:S(2)}) copy-start(s32[96]{0:T(128)} %param.7) | copy-start | bytes 1156
  27.9 22.2 %copy-start.1 = (f32[8,4224]{1,0:T(8,128)}, f32[8,4224]{1,0:T(8,128)S(1)}, u32[]{:S(2)}) copy-start(f32[8,4224]{1,0:T(8,128)S(1)} %collective-permute-done.1.head_ref) | copy-start | bytes 405508
  59.9 3.9 %copy-start.2 = (f32[384,48]{0,1:T(8,128)S(1)}, f32[384,48]{0,1:T(8,128)}, u32[]{:S(2)}) copy-start(f32[384,48]{0,1:T(8,128)} %param.6) | copy-start | bytes 221188
  59.9 28.9 %all-to-all-start.1 = ((f32[128,24,128]{2,1,0:T(8,128)}), f32[128,24,128]{2,1,0:T(8,128)S(1)}, u32[]{:S(2)}, u32[]{:S(2)}) async-start(f32[128,24,128]{2,1,0:T(8,128)} %bitcast.31), calls=%async_computation.1 | async-start | bytes 3145728 | tf_op jit(solution)/shard_map/all_to_all | solution.py:629
  63.9 24.9 %copy-start = (f32[2,2,256,384]{3,2,1,0:T(8,128)S(1)}, f32[2,2,256,384]{3,2,1,0:T(8,128)}, u32[]{:S(2)}) copy-start(f32[2,2,256,384]{3,2,1,0:T(8,128)} %param.5) | copy-start | bytes 4718596

commit v4 on v3

--- a/solution.py
+++ b/solution.py
@@ -19,7 +19,7 @@
 FRAMES = SHOTS + HALO
 GROUP = 128
 ROWS = 26
-PACK_CHUNKS = 8
+PACK_CHUNKS = 4
 ORDER = (0, 2, 1, 3)
 RELAX = 0.25
 RIDGE = 0.001
@@ -340,25 +340,31 @@
         for a in range(4):
             w_ref[pl.ds(aligned(a * rows_local + base, NODES), band), :] = parts[a]
 
-    def emit(n):
-        parts = [w_ref[pl.ds(a * rows_local + n, SHOTS, stride=NODES), :] for a in range(4)]
-        outs = []
-        for j in range(2):
-            co = RELAX * cos_ref[HALO : HALO + SHOTS, j * 128 : (j + 1) * 128]
-            si = RELAX * sin_ref[HALO : HALO + SHOTS, j * 128 : (j + 1) * 128]
-            re, im = parts[2 * j], parts[2 * j + 1]
-            outs += [re * co - im * si, im * co + re * si]
-        for a in range(3):
-            block = jnp.concatenate([outs[a], outs[3][32 * a : 32 * a + 32]], 0).T
+    def spectrum(n, a, first, size):
+        j = a // 2
+        re, im = w_ref[pl.ds(2 * j * rows_local + n + first * NODES, size, stride=NODES), :], w_ref[
+            pl.ds((2 * j + 1) * rows_local + n + first * NODES, size, stride=NODES), :
+        ]
+        shots = slice(HALO + first, HALO + first + size)
+        co = RELAX * cos_ref[shots, j * 128 : (j + 1) * 128]
+        si = RELAX * sin_ref[shots, j * 128 : (j + 1) * 128]
+        return re * co - im * si if a % 2 == 0 else im * co + re * si
+
+    sends = []
+    for a in range(3):
+        for n in range(NODES):
+            block = jnp.concatenate([spectrum(n, a, 0, SHOTS), spectrum(n, 3, 32 * a, 32)], 0).T
             send_ref[pl.ds(a * NODES + n, GROUP, stride=24), :] = block
-
-    for n in range(NODES):
-        emit(n)
-
-    send = pltpu.make_async_copy(send_ref, send_hbm, send_sem)
-    send.start()
+        part = pl.ds(a * NODES, NODES)
+        sends.append(
+            pltpu.make_async_copy(
+                send_ref.reshape(GROUP, 24, 128).at[:, part], send_hbm.reshape(GROUP, 24, 128).at[:, part], send_sem.at[a]
+            )
+        )
+        sends[-1].start()
     store.wait()
-    send.wait()
+    for send in sends:
+        send.wait()
 
 
 def signal(dither, last, recv, cos_t, sin_t, tables, head, gathers):
@@ -393,7 +399,7 @@
             pltpu.SemaphoreType.DMA,
             pltpu.SemaphoreType.DMA,
             pltpu.SemaphoreType.DMA,
-            pltpu.SemaphoreType.DMA,
+            pltpu.SemaphoreType.DMA((3,)),
             pltpu.SemaphoreType.DMA((4,)),
         ],
         compiler_params=pltpu.CompilerParams(vmem_limit_bytes=40 << 20),
@@ -543,12 +549,11 @@
         xh, xl = split(x)
         yh, yl = basis[j]
         low = dot(jnp.concatenate([yh, yl], 1), jnp.concatenate([xh, xh], 0)) + dot(yh, xl)
-        out_ref[2 * j] = low[:, :384]
-        out_ref[2 * j + 1] = low[:, 384:]
-        stores.append(
-            pltpu.make_async_copy(out_ref.at[pl.ds(2 * j, 2)], out_hbm.at[pl.ds(2 * j, 2)], out_sem.at[j])
-        )
-        stores[-1].start()
+        for c in range(2):
+            i = 2 * j + c
+            out_ref[i] = low[:, 384 * c : 384 * (c + 1)]
+            stores.append(pltpu.make_async_copy(out_ref.at[i], out_hbm.at[i], out_sem.at[i]))
+            stores[-1].start()
     for store in stores:
         store.wait()
 
@@ -566,7 +571,7 @@
             pltpu.VMEM((2, 256, 768), bf16),
             pltpu.VMEM((4, 256, 384), f32),
             pltpu.VMEM((768, 256), bf16),
-            pltpu.SemaphoreType.DMA((2,)),
+            pltpu.SemaphoreType.DMA((4,)),
             pltpu.SemaphoreType.DMA,
         ],
         compiler_params=pltpu.CompilerParams(vmem_limit_bytes=20 << 20),

time: 96.8 us -> 96.3 us (level)
  no operation moved by 1% of the time
where the time goes in v4:
time: 96.3 us; the launch traced here: 95.9 us
  waiting for transfers between devices  45.4 us (47%)
  starting transfers between devices  21.2 us (22%)
  Pallas kernels  20.7 us (21%)
  other arithmetic  6.38 us (7%)
  local copies, waits for them, and re-layouts  1.08 us (1%)
  between operations  1.02 us (1%)
    all_to_all x1, waiting for transfers between devices, shards(): lax.all_to_all(back.reshape(GROUP, 24, 128), ('node', 'freq'), split_axis...  23.8 us
    all_to_all x1, waiting for transfers between devices, shards(): lax.all_to_all(send, ('node', 'freq'), split_axis=0, concat_axis=0, tiled...  21.6 us
    all_to_all x1, starting transfers between devices, shards(): lax.all_to_all(send, ('node', 'freq'), split_axis=0, concat_axis=0, tiled...  11.4 us
    pallas_call x1, Pallas kernels, signal(): pl.pallas_call(signal_kernel, in_specs=[smem, smem, vmem, vmem, vmem, hbm...  9.57 us
    pallas_call x1, Pallas kernels, rank_reduce(): pl.pallas_call(rank_kernel, in_specs=[vmem, vmem, hbm], out_specs=hbm, ou...  7.47 us
    ppermute x1, starting transfers between devices, shards(): release_before = lax.ppermute(release_sample[SHOTS - HALO:], 'freq', up)  4.65 us
    all_to_all x1, starting transfers between devices, shards(): lax.all_to_all(back.reshape(GROUP, 24, 128), ('node', 'freq'), split_axis...  3.9 us
    pallas_call x1, Pallas kernels, pack(): pl.pallas_call(pack_kernel, in_specs=[hbm], out_specs=hbm, out_shape=pltp...  3.68 us
  transfers between devices with their start and end apart: 4, of which 2 were waited for; matrix products, arithmetic and copies ran while one was open for 6% of the time, Pallas kernels for 4%

profile of v4, /device:TPU:1, one launch (start us, length us, event | category | flops | bytes accessed | tf_op | source)
XLA Modules:
  0.0 95.9 jit_solution(8315297489541129078)
XLA Ops:
  0.6 0.8 fusion.33
  1.4 0.9 slice.45
  2.4 1.3 %collective-permute-start.1 = (f32[8,4224]{1,0:T(8,128)S(1)}, f32[8,4224]{1,0:T(8,128)S(1)}, u32[]{:S(2)}, u32[]{:S(2)}) collective-permute-start(f32[8,4224]{1,0:T(8,128)S(1)} %pad_maximum_fusion.3), channel_id=1, source_target_pairs={{1,0},{2,1},{3,2},{5,4},{6,5},{7,6},{9,8},{10,9},{11,10},{13,12},{... | collective-permute-start | bytes 405512 | tf_op jit(solution)/shard_map/ppermute | solution.py:620
  3.7 4.6 %collective-permute-start = (s32[4]{0:T(128)S(1)}, s32[4]{0:T(128)S(1)}, u32[]{:S(2)}, u32[]{:S(2)}) collective-permute-start(s32[4]{0:T(128)S(1)} %get-tuple-element.64), channel_id=1, source_target_pairs={{0,1},{1,2},{2,3},{4,5},{5,6},{6,7},{8,9},{9,10},{10,11},{12,13},{... | collective-permute-start | bytes 56 | tf_op jit(solution)/shard_map/ppermute | solution.py:623
  8.3 3.7 %pack.1 = f32[3328,128]{1,0:T(8,128)} custom-call(f32[4,32,8,384]{3,2,1,0:T(8,128)} %bitcast.25), custom_call_target="tpu_custom_call" | custom-call | tf_op jit(solution)/shard_map/pack/pallas_call | solution.py:124
  12.0 11.4 %all-to-all-start = ((f32[128,13,2,128]{3,2,1,0:T(2,128)}), f32[128,13,2,128]{3,2,1,0:T(2,128)S(1)}, u32[]{:S(2)}, u32[]{:S(2)}) async-start(f32[128,13,2,128]{3,2,1,0:T(2,128)} %bitcast.28), calls=%async_computation | async-start | bytes 3407872 | tf_op jit(solution)/shard_map/all_to_all | solution.py:615
  23.5 0.6 sine_multiply_fusion
  24.1 0.1 fusion.22
  24.2 0.3 sine_multiply_fusion.1
  24.6 0.1 fusion.20
  24.7 0.3 multiply_subtract_fusion.4
  25.2 1.1 %fusion = (bf16[2,256,512]{2,1,0:T(8,128)(2,1)}, bf16[2,256,512]{2,1,0:T(8,128)(2,1)}) fusion(f32[1,256,512]{2,1,0:T(8,128)S(1)} %maximum_bitcast_fusion.1, f32[1,256,512]{2,1,0:T(8,128)S(1)} %maximum_bitcast_fusion), kind=kLoop, calls=%fused_computation.4 | loop fusion | flops 1310720 | bytes 2097152 | tf_op jit(solution)/shard_map/convert_element_type | solution.py:608
  26.3 0.0 copy-start.3
  26.3 0.1 multiply_subtract_fusion
  26.4 1.1 %fusion.1 = (bf16[2,512,256]{2,1,0:T(8,128)(2,1)}, bf16[2,512,256]{2,1,0:T(8,128)(2,1)}) fusion(f32[1,512,256]{2,1,0:T(8,128)S(1)} %bitcast.30, f32[1,512,256]{2,1,0:T(8,128)S(1)} %bitcast.29), kind=kLoop, calls=%fused_computation.5 | loop fusion | flops 1310720 | bytes 2097152 | tf_op jit(solution)/shard_map/convert_element_type | solution.py:608
  27.6 0.0 collective-permute-done.1.head_ref
  27.6 0.0 copy-start.1
  27.6 0.0 collective-permute-done
  27.6 0.0 copy-done.3
  27.6 0.1 multiply_add_fusion.2
  27.7 0.5 fusion.12
  28.2 21.6 %all-to-all-done = f32[128,13,2,128]{3,2,1,0:T(2,128)S(1)} async-done(((f32[128,13,2,128]{3,2,1,0:T(2,128)}), f32[128,13,2,128]{3,2,1,0:T(2,128)S(1)}, u32[]{:S(2)}, u32[]{:S(2)}) %all-to-all-start) | async-done | bytes 1703968 | tf_op jit(solution)/shard_map/all_to_all | solution.py:615
  49.8 0.0 copy-done.1
  49.8 9.6 %signal.1 = (f32[8,98304]{1,0:T(8,128)}, f32[3072,128]{1,0:T(8,128)}) custom-call(s32[104]{0:T(128)S(1)} %get-tuple-element.23.d_ref, s32[1]{0:T(128)} %bitcast.1.last_ref, f32[3328,128]{1,0:T(8,128)S(1)} %bitcast.24, f32[104,256]{1,0:T(8,128)S(1)} %get-tuple-element.63.cos_ref, f32[104,256]{1,0:T(8,128)S(1)} %get-tuple-element.62.sin_ref, ...), custom_call_target="tpu_custom_call" | custom-call | tf_op jit(solution)/shard_map/signal/pallas_call | solution.py:375
  59.4 0.0 copy-start.2
  59.4 3.9 %all-to-all-start.1 = ((f32[128,24,128]{2,1,0:T(8,128)}), f32[128,24,128]{2,1,0:T(8,128)S(1)}, u32[]{:S(2)}, u32[]{:S(2)}) async-start(f32[128,24,128]{2,1,0:T(8,128)} %bitcast.31), calls=%async_computation.1 | async-start | bytes 3145728 | tf_op jit(solution)/shard_map/all_to_all | solution.py:634
  63.3 0.0 copy-done.2
  63.3 0.0 copy-start
  63.3 0.1 copy.7
  63.5 0.1 reduce-precision_convert_fusion.2
  63.6 0.8 pad_maximum_fusion.2.w_hbm
  64.4 23.8 %all-to-all-done.1 = f32[128,24,128]{2,1,0:T(8,128)S(1)} async-done(((f32[128,24,128]{2,1,0:T(8,128)}), f32[128,24,128]{2,1,0:T(8,128)S(1)}, u32[]{:S(2)}, u32[]{:S(2)}) %all-to-all-start.1) | async-done | bytes 1572896 | tf_op jit(solution)/shard_map/all_to_all | solution.py:634
  88.2 0.0 copy-done
  88.2 7.5 %rank.1 = f32[4,256,384]{2,1,0:T(8,128)} custom-call(f32[3072,128]{1,0:T(8,128)S(1)} %bitcast.27, f32[4,256,384]{2,1,0:T(8,128)S(1)} %bitcast.26, bf16[768,256]{1,0:T(8,128)(2,1)} %pad_maximum_fusion.2.w_hbm), custom_call_target="tpu_custom_call" | custom-call | tf_op jit(solution)/shard_map/rank/pallas_call | solution.py:564
  (12 shorter events, 0.2 us)
Async XLA Ops:
  2.4 25.2 %collective-permute-start.1 = (f32[8,4224]{1,0:T(8,128)S(1)}, f32[8,4224]{1,0:T(8,128)S(1)}, u32[]{:S(2)}, u32[]{:S(2)}) collective-permute-start(f32[8,4224]{1,0:T(8,128)S(1)} %pad_maximum_fusion.3), channel_id=1, source_target_pairs={{1,0},{2,1},{3,2},{5,4},{6,5},{7,6},{9,8},{10,9},{11,10},{13,12},{... | collective-permute-start | bytes 405512 | tf_op jit(solution)/shard_map/ppermute | solution.py:620
  3.7 23.9 %collective-permute-start = (s32[4]{0:T(128)S(1)}, s32[4]{0:T(128)S(1)}, u32[]{:S(2)}, u32[]{:S(2)}) collective-permute-start(s32[4]{0:T(128)S(1)} %get-tuple-element.64), channel_id=1, source_target_pairs={{0,1},{1,2},{2,3},{4,5},{5,6},{6,7},{8,9},{9,10},{10,11},{12,13},{... | collective-permute-start | bytes 56 | tf_op jit(solution)/shard_map/ppermute | solution.py:623
  12.0 37.8 %all-to-all-start = ((f32[128,13,2,128]{3,2,1,0:T(2,128)}), f32[128,13,2,128]{3,2,1,0:T(2,128)S(1)}, u32[]{:S(2)}, u32[]{:S(2)}) async-start(f32[128,13,2,128]{3,2,1,0:T(2,128)} %bitcast.28), calls=%async_computation | async-start | bytes 3407872 | tf_op jit(solution)/shard_map/all_to_all | solution.py:615
  26.3 1.3 %copy-start.3 = (s32[96]{0:T(128)S(1)}, s32[96]{0:T(128)}, u32[]{:S(2)}) copy-start(s32[96]{0:T(128)} %param.7) | copy-start | bytes 1156
  27.6 22.2 %copy-start.1 = (f32[8,4224]{1,0:T(8,128)}, f32[8,4224]{1,0:T(8,128)S(1)}, u32[]{:S(2)}) copy-start(f32[8,4224]{1,0:T(8,128)S(1)} %collective-permute-done.1.head_ref) | copy-start | bytes 405508
  59.4 3.9 %copy-start.2 = (f32[384,48]{0,1:T(8,128)S(1)}, f32[384,48]{0,1:T(8,128)}, u32[]{:S(2)}) copy-start(f32[384,48]{0,1:T(8,128)} %param.6) | copy-start | bytes 221188
  59.4 28.9 %all-to-all-start.1 = ((f32[128,24,128]{2,1,0:T(8,128)}), f32[128,24,128]{2,1,0:T(8,128)S(1)}, u32[]{:S(2)}, u32[]{:S(2)}) async-start(f32[128,24,128]{2,1,0:T(8,128)} %bitcast.31), calls=%async_computation.1 | async-start | bytes 3145728 | tf_op jit(solution)/shard_map/all_to_all | solution.py:634
  63.3 24.9 %copy-start = (f32[2,2,256,384]{3,2,1,0:T(8,128)S(1)}, f32[2,2,256,384]{3,2,1,0:T(8,128)}, u32[]{:S(2)}) copy-start(f32[2,2,256,384]{3,2,1,0:T(8,128)} %param.5) | copy-start | bytes 4718596

commit v5 on v4

--- a/solution.py
+++ b/solution.py
@@ -466,7 +466,7 @@
     for j in range(2):
         yy = dot(ah_ref[j], w_ref[...])
         y = yy[:, :128] + yy[:, 128:] + dot(al_ref[j], w_ref[:, :128])
-        basis.append(split(y))
+        basis.append(y)
         yt = y.T
         g = jnp.dot(yt, y, precision=highest, preferred_element_type=f32)
         g = g[:64] + flip * pltpu.roll(g[64:], 64, axis=1)
@@ -474,9 +474,11 @@
         g = jnp.where(diagonal, g + RIDGE * trace / RANK, g)
         eye = jnp.where(diagonal, 1.0, 0.0).astype(f32)
         systems.append([g[:RANK], eye[:RANK]])
-        yh, yl = split(yt)
-        c = dot(jnp.concatenate([yh, yl], 0), ah_ref[j])
-        c = c[:128] + c[128:] + dot(yh, al_ref[j])
+        yh, ym = split(yt)
+        yl = (yt - yh.astype(f32) - ym.astype(f32)).astype(bf16)
+        c = dot(jnp.concatenate([yh, ym, yl], 0), ah_ref[j])
+        rest = dot(jnp.concatenate([yh, ym], 0), al_ref[j])
+        c = c[:128] + ((c[128:256] + rest[:128]) + (c[256:] + rest[128:]))
         rights.append(jnp.concatenate([c[:64, :384] + c[64:, 384:], c[:64, 384:] - c[64:, :384]], 0))
 
     neg = jnp.where(lax.broadcasted_iota(jnp.int32, (NODES, 128), 1) < 64, -1.0, 1.0).astype(f32)
@@ -530,11 +532,6 @@
                 ws[i] = ws[i] - ((f0r * w0 + f0i * w0i) + (f1r * w1 + f1i * w1i))
     systems = [[jnp.concatenate(gs, 0), jnp.concatenate(ws, 0)] for gs, ws in state]
 
-    def two(left, right):
-        lh, ll = split(left)
-        rh, rl = split(right)
-        return dot(jnp.concatenate([lh, ll], 1), jnp.concatenate([rh, rh], 0)) + dot(lh, rl)
-
     stores = []
     for j in range(2):
         g, w = systems[j]
@@ -542,13 +539,15 @@
         w = w * lax.rsqrt(d)
         w = jnp.concatenate([w, jnp.zeros((16, 128), f32)], 0)
         left = jnp.concatenate([flip * w, pltpu.roll(w, 64, axis=1)], 0)
-        x = two(left.T, two(left, rights[j]))
-        x = jnp.concatenate(
-            [jnp.concatenate([x[:64], -x[64:]], 0), jnp.concatenate([x[64:], x[:64]], 0)], 1
+        v = jnp.dot(left, rights[j], precision=highest, preferred_element_type=f32)
+        conj = jnp.concatenate([w, -flip * pltpu.roll(w, 64, axis=1)], 0)
+        z = jnp.dot(basis[j], conj.T, precision=highest, preferred_element_type=f32)
+        v = jnp.concatenate(
+            [jnp.concatenate([v[:64], v[64:]], 1), jnp.concatenate([-v[64:], v[:64]], 1)], 0
         )
-        xh, xl = split(x)
-        yh, yl = basis[j]
-        low = dot(jnp.concatenate([yh, yl], 1), jnp.concatenate([xh, xh], 0)) + dot(yh, xl)
+        vh, vl = split(v)
+        zh, zl = split(z)
+        low = dot(jnp.concatenate([zh, zl], 1), jnp.concatenate([vh, vh], 0)) + dot(zh, vl)
         for c in range(2):
             i = 2 * j + c
             out_ref[i] = low[:, 384 * c : 384 * (c + 1)]

time: 96.3 us -> 96.9 us (level)
  no operation moved by 1% of the time
where the time goes in v5:
time: 96.9 us; the launch traced here: 96.5 us
  waiting for transfers between devices  45.4 us (47%)
  Pallas kernels  21.4 us (22%)
  starting transfers between devices  21.2 us (22%)
  other arithmetic  6.38 us (7%)
  local copies, waits for them, and re-layouts  1.08 us (1%)
  between operations  1.02 us (1%)
    all_to_all x1, waiting for transfers between devices, shards(): lax.all_to_all(back.reshape(GROUP, 24, 128), ('node', 'freq'), split_axis...  23.8 us
    all_to_all x1, waiting for transfers between devices, shards(): lax.all_to_all(send, ('node', 'freq'), split_axis=0, concat_axis=0, tiled...  21.6 us
    all_to_all x1, starting transfers between devices, shards(): lax.all_to_all(send, ('node', 'freq'), split_axis=0, concat_axis=0, tiled...  11.4 us
    pallas_call x1, Pallas kernels, signal(): pl.pallas_call(signal_kernel, in_specs=[smem, smem, vmem, vmem, vmem, hbm...  9.57 us
    pallas_call x1, Pallas kernels, rank_reduce(): pl.pallas_call(rank_kernel, in_specs=[vmem, vmem, hbm], out_specs=hbm, ou...  8.11 us
    ppermute x1, starting transfers between devices, shards(): release_before = lax.ppermute(release_sample[SHOTS - HALO:], 'freq', up)  4.65 us
    all_to_all x1, starting transfers between devices, shards(): lax.all_to_all(back.reshape(GROUP, 24, 128), ('node', 'freq'), split_axis...  3.9 us
    pallas_call x1, Pallas kernels, pack(): pl.pallas_call(pack_kernel, in_specs=[hbm], out_specs=hbm, out_shape=pltp...  3.68 us
  transfers between devices with their start and end apart: 4, of which 2 were waited for; matrix products, arithmetic and copies ran while one was open for 6% of the time, Pallas kernels for 4%

profile of v5, /device:TPU:1, one launch (start us, length us, event | category | flops | bytes accessed | tf_op | source)
XLA Modules:
  0.0 96.5 jit_solution(203308414354412370)
XLA Ops:
  0.6 0.8 fusion.33
  1.4 0.9 slice.45
  2.4 1.3 %collective-permute-start.1 = (f32[8,4224]{1,0:T(8,128)S(1)}, f32[8,4224]{1,0:T(8,128)S(1)}, u32[]{:S(2)}, u32[]{:S(2)}) collective-permute-start(f32[8,4224]{1,0:T(8,128)S(1)} %pad_maximum_fusion.3), channel_id=1, source_target_pairs={{1,0},{2,1},{3,2},{5,4},{6,5},{7,6},{9,8},{10,9},{11,10},{13,12},{... | collective-permute-start | bytes 405512 | tf_op jit(solution)/shard_map/ppermute | solution.py:619
  3.7 4.6 %collective-permute-start = (s32[4]{0:T(128)S(1)}, s32[4]{0:T(128)S(1)}, u32[]{:S(2)}, u32[]{:S(2)}) collective-permute-start(s32[4]{0:T(128)S(1)} %get-tuple-element.64), channel_id=1, source_target_pairs={{0,1},{1,2},{2,3},{4,5},{5,6},{6,7},{8,9},{9,10},{10,11},{12,13},{... | collective-permute-start | bytes 56 | tf_op jit(solution)/shard_map/ppermute | solution.py:622
  8.3 3.7 %pack.1 = f32[3328,128]{1,0:T(8,128)} custom-call(f32[4,32,8,384]{3,2,1,0:T(8,128)} %bitcast.25), custom_call_target="tpu_custom_call" | custom-call | tf_op jit(solution)/shard_map/pack/pallas_call | solution.py:124
  12.0 11.4 %all-to-all-start = ((f32[128,13,2,128]{3,2,1,0:T(2,128)}), f32[128,13,2,128]{3,2,1,0:T(2,128)S(1)}, u32[]{:S(2)}, u32[]{:S(2)}) async-start(f32[128,13,2,128]{3,2,1,0:T(2,128)} %bitcast.28), calls=%async_computation | async-start | bytes 3407872 | tf_op jit(solution)/shard_map/all_to_all | solution.py:614
  23.5 0.6 sine_multiply_fusion
  24.1 0.1 fusion.22
  24.2 0.3 sine_multiply_fusion.1
  24.6 0.1 fusion.20
  24.7 0.3 multiply_subtract_fusion.4
  25.2 1.1 %fusion = (bf16[2,256,512]{2,1,0:T(8,128)(2,1)}, bf16[2,256,512]{2,1,0:T(8,128)(2,1)}) fusion(f32[1,256,512]{2,1,0:T(8,128)S(1)} %maximum_bitcast_fusion.1, f32[1,256,512]{2,1,0:T(8,128)S(1)} %maximum_bitcast_fusion), kind=kLoop, calls=%fused_computation.4 | loop fusion | flops 1310720 | bytes 2097152 | tf_op jit(solution)/shard_map/convert_element_type | solution.py:607
  26.3 0.0 copy-start.3
  26.3 0.1 multiply_subtract_fusion
  26.4 1.1 %fusion.1 = (bf16[2,512,256]{2,1,0:T(8,128)(2,1)}, bf16[2,512,256]{2,1,0:T(8,128)(2,1)}) fusion(f32[1,512,256]{2,1,0:T(8,128)S(1)} %bitcast.30, f32[1,512,256]{2,1,0:T(8,128)S(1)} %bitcast.29), kind=kLoop, calls=%fused_computation.5 | loop fusion | flops 1310720 | bytes 2097152 | tf_op jit(solution)/shard_map/convert_element_type | solution.py:607
  27.6 0.0 collective-permute-done.1.head_ref
  27.6 0.0 copy-start.1
  27.6 0.0 collective-permute-done
  27.6 0.0 copy-done.3
  27.6 0.1 multiply_add_fusion.2
  27.7 0.5 fusion.12
  28.2 21.6 %all-to-all-done = f32[128,13,2,128]{3,2,1,0:T(2,128)S(1)} async-done(((f32[128,13,2,128]{3,2,1,0:T(2,128)}), f32[128,13,2,128]{3,2,1,0:T(2,128)S(1)}, u32[]{:S(2)}, u32[]{:S(2)}) %all-to-all-start) | async-done | bytes 1703968 | tf_op jit(solution)/shard_map/all_to_all | solution.py:614
  49.8 0.0 copy-done.1
  49.8 9.6 %signal.1 = (f32[8,98304]{1,0:T(8,128)}, f32[3072,128]{1,0:T(8,128)}) custom-call(s32[104]{0:T(128)S(1)} %get-tuple-element.23.d_ref, s32[1]{0:T(128)} %bitcast.1.last_ref, f32[3328,128]{1,0:T(8,128)S(1)} %bitcast.24, f32[104,256]{1,0:T(8,128)S(1)} %get-tuple-element.63.cos_ref, f32[104,256]{1,0:T(8,128)S(1)} %get-tuple-element.62.sin_ref, ...), custom_call_target="tpu_custom_call" | custom-call | tf_op jit(solution)/shard_map/signal/pallas_call | solution.py:375
  59.4 0.0 copy-start.2
  59.4 3.9 %all-to-all-start.1 = ((f32[128,24,128]{2,1,0:T(8,128)}), f32[128,24,128]{2,1,0:T(8,128)S(1)}, u32[]{:S(2)}, u32[]{:S(2)}) async-start(f32[128,24,128]{2,1,0:T(8,128)} %bitcast.31), calls=%async_computation.1 | async-start | bytes 3145728 | tf_op jit(solution)/shard_map/all_to_all | solution.py:633
  63.3 0.0 copy-done.2
  63.3 0.0 copy-start
  63.3 0.1 copy.7
  63.5 0.1 reduce-precision_convert_fusion.2
  63.6 0.8 pad_maximum_fusion.2.w_hbm
  64.4 23.8 %all-to-all-done.1 = f32[128,24,128]{2,1,0:T(8,128)S(1)} async-done(((f32[128,24,128]{2,1,0:T(8,128)}), f32[128,24,128]{2,1,0:T(8,128)S(1)}, u32[]{:S(2)}, u32[]{:S(2)}) %all-to-all-start.1) | async-done | bytes 1572896 | tf_op jit(solution)/shard_map/all_to_all | solution.py:633
  88.2 0.0 copy-done
  88.2 8.1 %rank.1 = f32[4,256,384]{2,1,0:T(8,128)} custom-call(f32[3072,128]{1,0:T(8,128)S(1)} %bitcast.27, f32[4,256,384]{2,1,0:T(8,128)S(1)} %bitcast.26, bf16[768,256]{1,0:T(8,128)(2,1)} %pad_maximum_fusion.2.w_hbm), custom_call_target="tpu_custom_call" | custom-call | tf_op jit(solution)/shard_map/rank/pallas_call | solution.py:563
  (12 shorter events, 0.2 us)
Async XLA Ops:
  2.4 25.2 %collective-permute-start.1 = (f32[8,4224]{1,0:T(8,128)S(1)}, f32[8,4224]{1,0:T(8,128)S(1)}, u32[]{:S(2)}, u32[]{:S(2)}) collective-permute-start(f32[8,4224]{1,0:T(8,128)S(1)} %pad_maximum_fusion.3), channel_id=1, source_target_pairs={{1,0},{2,1},{3,2},{5,4},{6,5},{7,6},{9,8},{10,9},{11,10},{13,12},{... | collective-permute-start | bytes 405512 | tf_op jit(solution)/shard_map/ppermute | solution.py:619
  3.7 23.9 %collective-permute-start = (s32[4]{0:T(128)S(1)}, s32[4]{0:T(128)S(1)}, u32[]{:S(2)}, u32[]{:S(2)}) collective-permute-start(s32[4]{0:T(128)S(1)} %get-tuple-element.64), channel_id=1, source_target_pairs={{0,1},{1,2},{2,3},{4,5},{5,6},{6,7},{8,9},{9,10},{10,11},{12,13},{... | collective-permute-start | bytes 56 | tf_op jit(solution)/shard_map/ppermute | solution.py:622
  12.0 37.8 %all-to-all-start = ((f32[128,13,2,128]{3,2,1,0:T(2,128)}), f32[128,13,2,128]{3,2,1,0:T(2,128)S(1)}, u32[]{:S(2)}, u32[]{:S(2)}) async-start(f32[128,13,2,128]{3,2,1,0:T(2,128)} %bitcast.28), calls=%async_computation | async-start | bytes 3407872 | tf_op jit(solution)/shard_map/all_to_all | solution.py:614
  26.3 1.3 %copy-start.3 = (s32[96]{0:T(128)S(1)}, s32[96]{0:T(128)}, u32[]{:S(2)}) copy-start(s32[96]{0:T(128)} %param.7) | copy-start | bytes 1156
  27.6 22.2 %copy-start.1 = (f32[8,4224]{1,0:T(8,128)}, f32[8,4224]{1,0:T(8,128)S(1)}, u32[]{:S(2)}) copy-start(f32[8,4224]{1,0:T(8,128)S(1)} %collective-permute-done.1.head_ref) | copy-start | bytes 405508
  59.4 3.9 %copy-start.2 = (f32[384,48]{0,1:T(8,128)S(1)}, f32[384,48]{0,1:T(8,128)}, u32[]{:S(2)}) copy-start(f32[384,48]{0,1:T(8,128)} %param.6) | copy-start | bytes 221188
  59.4 28.9 %all-to-all-start.1 = ((f32[128,24,128]{2,1,0:T(8,128)}), f32[128,24,128]{2,1,0:T(8,128)S(1)}, u32[]{:S(2)}, u32[]{:S(2)}) async-start(f32[128,24,128]{2,1,0:T(8,128)} %bitcast.31), calls=%async_computation.1 | async-start | bytes 3145728 | tf_op jit(solution)/shard_map/all_to_all | solution.py:633
  63.3 24.9 %copy-start = (f32[2,2,256,384]{3,2,1,0:T(8,128)S(1)}, f32[2,2,256,384]{3,2,1,0:T(8,128)}, u32[]{:S(2)}) copy-start(f32[2,2,256,384]{3,2,1,0:T(8,128)} %param.5) | copy-start | bytes 4718596

commit v6 on v5

--- a/solution.py
+++ b/solution.py
@@ -160,8 +160,13 @@
     ]
     loads[0].start()
     loads[1].start()
-    fetch = pltpu.make_async_copy(gath_ref, g_ref.at[:, pl.ds(0, local)], in_sem)
-    fetch.start()
+    middle = FRAMES // 2 * FRAME
+    fetches = [
+        pltpu.make_async_copy(gath_ref.at[:, pl.ds(x, n)], g_ref.at[:, pl.ds(x, n)], in_sem.at[i])
+        for i, (x, n) in enumerate([(0, middle), (middle, local - middle)])
+    ]
+    for fetch in fetches:
+        fetch.start()
     fetch_head = pltpu.make_async_copy(head_ref.at[:, pl.ds(0, HALO * FRAME)], g_ref.at[:, pl.ds(local, HALO * FRAME)], head_sem)
     fetch_head.start()
     loads[2].start()
@@ -253,12 +258,14 @@
     for i in range(rows_frames // step):
         build(i)
 
-    fetch.wait()
-    fetch_head.wait()
     half_frames = rows_frames // 2
 
     for i in range(4):
         m, c = i // 2, i % 2
+        if c == 0:
+            fetches[m].wait()
+        if i == 2:
+            fetch_head.wait()
         even, odd = pair(aligned(m * half_frames, 16), half_frames, c)
         upper, lower = columns(c)
         for f in range(FRAMES // 2):
@@ -396,7 +403,7 @@
             pltpu.VMEM((2, 256, 512), bf16),
             pltpu.VMEM((2, 512, 256), bf16),
             pltpu.VMEM((2, 512, 256), bf16),
-            pltpu.SemaphoreType.DMA,
+            pltpu.SemaphoreType.DMA((2,)),
             pltpu.SemaphoreType.DMA,
             pltpu.SemaphoreType.DMA,
             pltpu.SemaphoreType.DMA((3,)),

time: 96.9 us -> 97.1 us (level)
  no operation moved by 1% of the time
where the time goes in v6:
time: 97.1 us; the launch traced here: 96.8 us
  waiting for transfers between devices  45.4 us (47%)
  Pallas kernels  21.6 us (22%)
  starting transfers between devices  21.2 us (22%)
  other arithmetic  6.38 us (7%)
  local copies, waits for them, and re-layouts  1.08 us (1%)
  between operations  1.02 us (1%)
    all_to_all x1, waiting for transfers between devices, shards(): lax.all_to_all(back.reshape(GROUP, 24, 128), ('node', 'freq'), split_axis...  23.9 us
    all_to_all x1, waiting for transfers between devices, shards(): lax.all_to_all(send, ('node', 'freq'), split_axis=0, concat_axis=0, tiled...  21.6 us
    all_to_all x1, starting transfers between devices, shards(): lax.all_to_all(send, ('node', 'freq'), split_axis=0, concat_axis=0, tiled...  11.4 us
    pallas_call x1, Pallas kernels, signal(): pl.pallas_call(signal_kernel, in_specs=[smem, smem, vmem, vmem, vmem, hbm...  9.82 us
    pallas_call x1, Pallas kernels, rank_reduce(): pl.pallas_call(rank_kernel, in_specs=[vmem, vmem, hbm], out_specs=hbm, ou...  8.1 us
    ppermute x1, starting transfers between devices, shards(): release_before = lax.ppermute(release_sample[SHOTS - HALO:], 'freq', up)  4.65 us
    all_to_all x1, starting transfers between devices, shards(): lax.all_to_all(back.reshape(GROUP, 24, 128), ('node', 'freq'), split_axis...  3.9 us
    pallas_call x1, Pallas kernels, pack(): pl.pallas_call(pack_kernel, in_specs=[hbm], out_specs=hbm, out_shape=pltp...  3.68 us
  transfers between devices with their start and end apart: 4, of which 2 were waited for; matrix products, arithmetic and copies ran while one was open for 6% of the time, Pallas kernels for 4%

profile of v6, /device:TPU:1, one launch (start us, length us, event | category | flops | bytes accessed | tf_op | source)
XLA Modules:
  0.0 96.8 jit_solution(10844298409213725839)
XLA Ops:
  0.6 0.8 fusion.33
  1.4 0.9 slice.45
  2.4 1.3 %collective-permute-start.1 = (f32[8,4224]{1,0:T(8,128)S(1)}, f32[8,4224]{1,0:T(8,128)S(1)}, u32[]{:S(2)}, u32[]{:S(2)}) collective-permute-start(f32[8,4224]{1,0:T(8,128)S(1)} %pad_maximum_fusion.3), channel_id=1, source_target_pairs={{1,0},{2,1},{3,2},{5,4},{6,5},{7,6},{9,8},{10,9},{11,10},{13,12},{... | collective-permute-start | bytes 405512 | tf_op jit(solution)/shard_map/ppermute | solution.py:626
  3.7 4.6 %collective-permute-start = (s32[4]{0:T(128)S(1)}, s32[4]{0:T(128)S(1)}, u32[]{:S(2)}, u32[]{:S(2)}) collective-permute-start(s32[4]{0:T(128)S(1)} %get-tuple-element.64), channel_id=1, source_target_pairs={{0,1},{1,2},{2,3},{4,5},{5,6},{6,7},{8,9},{9,10},{10,11},{12,13},{... | collective-permute-start | bytes 56 | tf_op jit(solution)/shard_map/ppermute | solution.py:629
  8.3 3.7 %pack.1 = f32[3328,128]{1,0:T(8,128)} custom-call(f32[4,32,8,384]{3,2,1,0:T(8,128)} %bitcast.25), custom_call_target="tpu_custom_call" | custom-call | tf_op jit(solution)/shard_map/pack/pallas_call | solution.py:124
  12.0 11.4 %all-to-all-start = ((f32[128,13,2,128]{3,2,1,0:T(2,128)}), f32[128,13,2,128]{3,2,1,0:T(2,128)S(1)}, u32[]{:S(2)}, u32[]{:S(2)}) async-start(f32[128,13,2,128]{3,2,1,0:T(2,128)} %bitcast.28), calls=%async_computation | async-start | bytes 3407872 | tf_op jit(solution)/shard_map/all_to_all | solution.py:621
  23.5 0.6 sine_multiply_fusion
  24.1 0.1 fusion.22
  24.2 0.3 sine_multiply_fusion.1
  24.6 0.1 fusion.20
  24.7 0.3 multiply_subtract_fusion.4
  25.2 1.1 %fusion = (bf16[2,256,512]{2,1,0:T(8,128)(2,1)}, bf16[2,256,512]{2,1,0:T(8,128)(2,1)}) fusion(f32[1,256,512]{2,1,0:T(8,128)S(1)} %maximum_bitcast_fusion.1, f32[1,256,512]{2,1,0:T(8,128)S(1)} %maximum_bitcast_fusion), kind=kLoop, calls=%fused_computation.4 | loop fusion | flops 1310720 | bytes 2097152 | tf_op jit(solution)/shard_map/convert_element_type | solution.py:614
  26.3 0.0 copy-start.3
  26.3 0.1 multiply_subtract_fusion
  26.4 1.1 %fusion.1 = (bf16[2,512,256]{2,1,0:T(8,128)(2,1)}, bf16[2,512,256]{2,1,0:T(8,128)(2,1)}) fusion(f32[1,512,256]{2,1,0:T(8,128)S(1)} %bitcast.30, f32[1,512,256]{2,1,0:T(8,128)S(1)} %bitcast.29), kind=kLoop, calls=%fused_computation.5 | loop fusion | flops 1310720 | bytes 2097152 | tf_op jit(solution)/shard_map/convert_element_type | solution.py:614
  27.6 0.0 collective-permute-done.1.head_ref
  27.6 0.0 copy-start.1
  27.6 0.0 collective-permute-done
  27.6 0.0 copy-done.3
  27.6 0.1 multiply_add_fusion.2
  27.7 0.5 fusion.12
  28.2 21.6 %all-to-all-done = f32[128,13,2,128]{3,2,1,0:T(2,128)S(1)} async-done(((f32[128,13,2,128]{3,2,1,0:T(2,128)}), f32[128,13,2,128]{3,2,1,0:T(2,128)S(1)}, u32[]{:S(2)}, u32[]{:S(2)}) %all-to-all-start) | async-done | bytes 1703968 | tf_op jit(solution)/shard_map/all_to_all | solution.py:621
  49.8 0.0 copy-done.1
  49.8 9.8 %signal.1 = (f32[8,98304]{1,0:T(8,128)}, f32[3072,128]{1,0:T(8,128)}) custom-call(s32[104]{0:T(128)S(1)} %get-tuple-element.23.d_ref, s32[1]{0:T(128)} %bitcast.1.last_ref, f32[3328,128]{1,0:T(8,128)S(1)} %bitcast.24, f32[104,256]{1,0:T(8,128)S(1)} %get-tuple-element.63.cos_ref, f32[104,256]{1,0:T(8,128)S(1)} %get-tuple-element.62.sin_ref, ...), custom_call_target="tpu_custom_call" | custom-call | tf_op jit(solution)/shard_map/signal/pallas_call | solution.py:382
  59.6 0.0 copy-start.2
  59.6 3.9 %all-to-all-start.1 = ((f32[128,24,128]{2,1,0:T(8,128)}), f32[128,24,128]{2,1,0:T(8,128)S(1)}, u32[]{:S(2)}, u32[]{:S(2)}) async-start(f32[128,24,128]{2,1,0:T(8,128)} %bitcast.31), calls=%async_computation.1 | async-start | bytes 3145728 | tf_op jit(solution)/shard_map/all_to_all | solution.py:640
  63.5 0.0 copy-done.2
  63.5 0.0 copy-start
  63.6 0.1 copy.7
  63.7 0.1 reduce-precision_convert_fusion.2
  63.8 0.8 pad_maximum_fusion.2.w_hbm
  64.6 23.9 %all-to-all-done.1 = f32[128,24,128]{2,1,0:T(8,128)S(1)} async-done(((f32[128,24,128]{2,1,0:T(8,128)}), f32[128,24,128]{2,1,0:T(8,128)S(1)}, u32[]{:S(2)}, u32[]{:S(2)}) %all-to-all-start.1) | async-done | bytes 1572896 | tf_op jit(solution)/shard_map/all_to_all | solution.py:640
  88.5 0.0 copy-done
  88.5 8.1 %rank.1 = f32[4,256,384]{2,1,0:T(8,128)} custom-call(f32[3072,128]{1,0:T(8,128)S(1)} %bitcast.27, f32[4,256,384]{2,1,0:T(8,128)S(1)} %bitcast.26, bf16[768,256]{1,0:T(8,128)(2,1)} %pad_maximum_fusion.2.w_hbm), custom_call_target="tpu_custom_call" | custom-call | tf_op jit(solution)/shard_map/rank/pallas_call | solution.py:570
  (12 shorter events, 0.2 us)
Async XLA Ops:
  2.4 25.2 %collective-permute-start.1 = (f32[8,4224]{1,0:T(8,128)S(1)}, f32[8,4224]{1,0:T(8,128)S(1)}, u32[]{:S(2)}, u32[]{:S(2)}) collective-permute-start(f32[8,4224]{1,0:T(8,128)S(1)} %pad_maximum_fusion.3), channel_id=1, source_target_pairs={{1,0},{2,1},{3,2},{5,4},{6,5},{7,6},{9,8},{10,9},{11,10},{13,12},{... | collective-permute-start | bytes 405512 | tf_op jit(solution)/shard_map/ppermute | solution.py:626
  3.7 23.9 %collective-permute-start = (s32[4]{0:T(128)S(1)}, s32[4]{0:T(128)S(1)}, u32[]{:S(2)}, u32[]{:S(2)}) collective-permute-start(s32[4]{0:T(128)S(1)} %get-tuple-element.64), channel_id=1, source_target_pairs={{0,1},{1,2},{2,3},{4,5},{5,6},{6,7},{8,9},{9,10},{10,11},{12,13},{... | collective-permute-start | bytes 56 | tf_op jit(solution)/shard_map/ppermute | solution.py:629
  12.0 37.8 %all-to-all-start = ((f32[128,13,2,128]{3,2,1,0:T(2,128)}), f32[128,13,2,128]{3,2,1,0:T(2,128)S(1)}, u32[]{:S(2)}, u32[]{:S(2)}) async-start(f32[128,13,2,128]{3,2,1,0:T(2,128)} %bitcast.28), calls=%async_computation | async-start | bytes 3407872 | tf_op jit(solution)/shard_map/all_to_all | solution.py:621
  26.3 1.3 %copy-start.3 = (s32[96]{0:T(128)S(1)}, s32[96]{0:T(128)}, u32[]{:S(2)}) copy-start(s32[96]{0:T(128)} %param.7) | copy-start | bytes 1156
  27.6 22.2 %copy-start.1 = (f32[8,4224]{1,0:T(8,128)}, f32[8,4224]{1,0:T(8,128)S(1)}, u32[]{:S(2)}) copy-start(f32[8,4224]{1,0:T(8,128)S(1)} %collective-permute-done.1.head_ref) | copy-start | bytes 405508
  59.6 3.9 %copy-start.2 = (f32[384,48]{0,1:T(8,128)S(1)}, f32[384,48]{0,1:T(8,128)}, u32[]{:S(2)}) copy-start(f32[384,48]{0,1:T(8,128)} %param.6) | copy-start | bytes 221188
  59.6 28.9 %all-to-all-start.1 = ((f32[128,24,128]{2,1,0:T(8,128)}), f32[128,24,128]{2,1,0:T(8,128)S(1)}, u32[]{:S(2)}, u32[]{:S(2)}) async-start(f32[128,24,128]{2,1,0:T(8,128)} %bitcast.31), calls=%async_computation.1 | async-start | bytes 3145728 | tf_op jit(solution)/shard_map/all_to_all | solution.py:640
  63.5 24.9 %copy-start = (f32[2,2,256,384]{3,2,1,0:T(8,128)S(1)}, f32[2,2,256,384]{3,2,1,0:T(8,128)}, u32[]{:S(2)}) copy-start(f32[2,2,256,384]{3,2,1,0:T(8,128)} %param.5) | copy-start | bytes 4718596
